TPU v7x, 128 devices: a whole 4x4x4 slice. The times are simulated.
128 devices in a mesh: dp: 8 (over z, core), seq: 16 (over y, x).
Axes of the slice: x: 4, y: 4, z: 4, core: 2. Of those that a mesh axis runs over, the one named last changes fastest.
Arguments:
- tokens: bfloat16 [16384, 2688], P(('dp', 'seq')), may hold values from -6 to 6
- q_weight: bfloat16 [2688, 4096], P('dp', 'seq'), may hold values from -0.125 to 0.125
- key_projection: bfloat16 [2688, 2048], P('dp', 'seq'), may hold values from -0.125 to 0.125
- value_projection: bfloat16 [2688, 2048], P('dp', 'seq'), may hold values from -0.125 to 0.125
- query_norm_gain: float32 [128], replicated, may hold values from 0.5 to 2.5
- key_norm_gain: float32 [128], replicated, may hold values from 0.5 to 2.5
- doc_lengths: int32 [8, 4], P('dp'), may hold values from 1 to 1536, 2048 in all within a row
- out_cot: bfloat16 [16384, 4096], P('dp', 'seq'), may hold values from -6 to 6
Outputs:
- attn_out: bfloat16 [16384, 4096], P(('dp', 'seq'))
- token_grad: bfloat16 [16384, 2688], P(('dp', 'seq'))
- q_weight_grad: float32 [2688, 4096], P('dp', 'seq')
- k_weight_grad: float32 [2688, 2048], P('dp', 'seq')
- v_weight_grad: float32 [2688, 2048], P('dp', 'seq')
Inputs may be any that keep to these rules, and one draw needn't show every extreme that they name: `doc_lengths`: each row's 4 lengths add up to 2048, and in every row the longest document has exactly 1536 tokens.
All inputs are finite; a program needn't handle non-finite values.
Results may differ from a plain program's by a relative error of at most 0.015.
Values may be sent and summed in bfloat16 or wider, within the bound.
A program may use at most 128 MiB of HBM per device.

v0:
```python
import jax
import jax.numpy as jnp
from jax import lax
from jax.sharding import PartitionSpec as P

HEAD_WIDTH = 128
WINDOW = 1024


score_scale = 168.0 ** (-0.5)
rope_base = 10000.0
norm_eps = 1e-06


def doc_layout(length_row, length):
    ends = jnp.cumsum(length_row, dtype=jnp.int32)
    starts = ends - length_row
    token = jnp.arange(length, dtype=jnp.int32)
    doc_index = jnp.sum(
        (token[:, None] >= ends[None, :]).astype(jnp.int32), axis=1, dtype=jnp.int32
    )
    member = doc_index[:, None] == jnp.arange(length_row.shape[0], dtype=jnp.int32)[None, :]
    position = token - jnp.sum(jnp.where(member, starts[None, :], 0), axis=1, dtype=jnp.int32)
    return (doc_index, position)


def rope_tables(position, head_size):
    half = head_size // 2
    inverse = rope_base ** (-jnp.arange(half, dtype=jnp.float32) * (2.0 / head_size))
    angle = position.astype(jnp.float32)[:, None] * inverse[None, :]
    cosine = jnp.concatenate([jnp.cos(angle), jnp.cos(angle)], axis=1)
    sine = jnp.concatenate([jnp.sin(angle), jnp.sin(angle)], axis=1)
    return (cosine, sine)


def norm_rotate(vectors, gain, cosine, sine):
    factor = lax.rsqrt(jnp.mean(vectors * vectors, axis=-1, keepdims=True) + norm_eps)
    normed = vectors * factor * gain
    half = vectors.shape[-1] // 2
    turned = jnp.concatenate([-normed[..., half:], normed[..., :half]], axis=-1)
    return normed * cosine[:, None, :] + turned * sine[:, None, :]


def shape_heads(
    projected_rows,
    query_norm_gain,
    key_norm_gain,
    cosine,
    sine,
    query_heads,
    value_heads,
    head_size,
):
    length = projected_rows.shape[0]
    query_cols = query_heads * head_size
    key_columns = value_heads * head_size
    queries = projected_rows[:, :query_cols].reshape(length, query_heads, head_size)
    keys = projected_rows[:, query_cols : query_cols + key_columns].reshape(
        length, value_heads, head_size
    )
    values = projected_rows[:, query_cols + key_columns :].reshape(length, value_heads, head_size)
    return (
        norm_rotate(queries, query_norm_gain, cosine, sine),
        norm_rotate(keys, key_norm_gain, cosine, sine),
        values,
    )


def band_mask(doc_index, query_start, key_start, query_rows, key_rows):
    query_pos = query_start + jnp.arange(query_rows, dtype=jnp.int32)
    key_pos = key_start + jnp.arange(key_rows, dtype=jnp.int32)
    query_doc = lax.dynamic_slice_in_dim(doc_index, query_start, query_rows, 0)
    key_doc = lax.dynamic_slice_in_dim(doc_index, key_start, key_rows, 0)
    spacing = query_pos[:, None] - key_pos[None, :]
    return (query_doc[:, None] == key_doc[None, :]) & (spacing >= 0) & (spacing < WINDOW)


def block_probs(query_part, key_part, allowed):
    scores = (
        jnp.einsum("qhgd,khd->hgqk", query_part, key_part, preferred_element_type=jnp.float32)
        * score_scale
    )
    weights = jnp.where(allowed[None, None], jnp.exp(scores), 0.0)
    return weights / jnp.sum(weights, axis=-1, keepdims=True)


def layer_kernel(
    projected_rows, length_row, cotangent, query_norm_gain, key_norm_gain, query_heads, value_heads
):
    length = projected_rows.shape[0]
    doc_index, position = doc_layout(length_row, length)
    cosine, sine = rope_tables(position, HEAD_WIDTH)
    (queries, keys, values), pull = jax.vjp(
        lambda inner: shape_heads(
            inner,
            query_norm_gain,
            key_norm_gain,
            cosine,
            sine,
            query_heads,
            value_heads,
            HEAD_WIDTH,
        ),
        projected_rows,
    )
    group = query_heads // value_heads
    query_bf = queries.astype(jnp.bfloat16).reshape(length, value_heads, group, HEAD_WIDTH)
    key_bf = keys.astype(jnp.bfloat16)
    value_bf = values.astype(jnp.bfloat16)
    grad_out = cotangent.reshape(length, value_heads, group, HEAD_WIDTH)
    query_rows = min(512, length)
    key_rows = min(length, query_rows + WINDOW)
    blocks = length // query_rows

    def block_view(index):
        index = index.astype(jnp.int32)
        query_start = index * query_rows
        key_start = jnp.maximum(query_start + query_rows - key_rows, 0)
        query_part = lax.dynamic_slice_in_dim(query_bf, query_start, query_rows, 0)
        key_part = lax.dynamic_slice_in_dim(key_bf, key_start, key_rows, 0)
        value_part = lax.dynamic_slice_in_dim(value_bf, key_start, key_rows, 0)
        allowed = band_mask(doc_index, query_start, key_start, query_rows, key_rows)
        return (
            query_start,
            key_start,
            query_part,
            key_part,
            value_part,
            block_probs(query_part, key_part, allowed),
        )

    def forward_block(index):
        _, _, _, _, value_part, probs = block_view(index)
        mixed = jnp.einsum(
            "hgqk,khd->qhgd",
            probs.astype(jnp.bfloat16),
            value_part,
            preferred_element_type=jnp.float32,
        )
        return mixed.astype(jnp.bfloat16).reshape(query_rows, query_heads * HEAD_WIDTH)

    head_output = lax.map(forward_block, jnp.arange(blocks, dtype=jnp.int32)).reshape(
        length, query_heads * HEAD_WIDTH
    )

    def backward_block(index, carry):
        grad_query, grad_key, grad_value = carry
        query_start, key_start, query_part, key_part, value_part, probs = block_view(index)
        grad_part = lax.dynamic_slice_in_dim(grad_out, query_start, query_rows, 0)
        probs_bf = probs.astype(jnp.bfloat16)
        value_term = jnp.einsum(
            "hgqk,qhgd->khd", probs_bf, grad_part, preferred_element_type=jnp.float32
        )
        grad_probs = jnp.einsum(
            "qhgd,khd->hgqk", grad_part, value_part, preferred_element_type=jnp.float32
        )
        delta = jnp.sum(probs * grad_probs, axis=-1, keepdims=True)
        grad_scores = (probs * (grad_probs - delta)).astype(jnp.bfloat16)
        query_term = (
            jnp.einsum("hgqk,khd->qhgd", grad_scores, key_part, preferred_element_type=jnp.float32)
            * score_scale
        )
        key_term = (
            jnp.einsum(
                "hgqk,qhgd->khd", grad_scores, query_part, preferred_element_type=jnp.float32
            )
            * score_scale
        )
        grad_query = lax.dynamic_update_slice_in_dim(grad_query, query_term, query_start, 0)
        grad_key = lax.dynamic_update_slice_in_dim(
            grad_key,
            lax.dynamic_slice_in_dim(grad_key, key_start, key_rows, 0) + key_term,
            key_start,
            0,
        )
        grad_value = lax.dynamic_update_slice_in_dim(
            grad_value,
            lax.dynamic_slice_in_dim(grad_value, key_start, key_rows, 0) + value_term,
            key_start,
            0,
        )
        return (grad_query, grad_key, grad_value)

    start_grads = (
        jnp.zeros((length, value_heads, group, HEAD_WIDTH), jnp.float32),
        jnp.zeros((length, value_heads, HEAD_WIDTH), jnp.float32),
        jnp.zeros((length, value_heads, HEAD_WIDTH), jnp.float32),
    )
    grad_query, grad_key, grad_value = lax.fori_loop(0, blocks, backward_block, start_grads)
    (projection_gradient,) = pull(
        (grad_query.reshape(length, query_heads, HEAD_WIDTH), grad_key, grad_value)
    )
    return (head_output, projection_gradient.astype(jnp.bfloat16))


def local(
    tokens,
    q_weight,
    key_projection,
    value_projection,
    query_norm_gain,
    key_norm_gain,
    doc_lengths,
    out_cot,
):
    query_whole, key_whole, value_whole = (
        lax.all_gather(q_weight, "dp", axis=0, tiled=True),
        lax.all_gather(key_projection, "dp", axis=0, tiled=True),
        lax.all_gather(value_projection, "dp", axis=0, tiled=True),
    )
    joined = jnp.concatenate([query_whole, key_whole, value_whole], axis=1)
    query_heads = q_weight.shape[1] // HEAD_WIDTH
    value_heads = key_projection.shape[1] // HEAD_WIDTH
    row_tokens = lax.all_gather(tokens, "seq", axis=0, tiled=True)
    projected_rows = jnp.dot(row_tokens, joined, preferred_element_type=jnp.float32)
    head_output, projection_gradient = layer_kernel(
        projected_rows,
        doc_lengths[0],
        out_cot,
        query_norm_gain,
        key_norm_gain,
        query_heads,
        value_heads,
    )
    attn_out = lax.all_to_all(head_output, "seq", split_axis=0, concat_axis=1, tiled=True)
    token_grad = lax.psum_scatter(
        lax.dot_general(
            projection_gradient,
            joined,
            (((1,), (1,)), ((), ())),
            preferred_element_type=jnp.float32,
        ).astype(jnp.bfloat16),
        "seq",
        scatter_dimension=0,
        tiled=True,
    )
    weight_terms = lax.dot_general(
        row_tokens,
        projection_gradient,
        (((0,), (0,)), ((), ())),
        preferred_element_type=jnp.float32,
    )
    query_cols = q_weight.shape[1]
    key_columns = key_projection.shape[1]
    query_grad, key_grad, value_grad = (
        lax.psum_scatter(
            weight_terms[:, :query_cols].astype(jnp.bfloat16), "dp", scatter_dimension=0, tiled=True
        ).astype(jnp.float32),
        lax.psum_scatter(
            weight_terms[:, query_cols : query_cols + key_columns].astype(jnp.bfloat16),
            "dp",
            scatter_dimension=0,
            tiled=True,
        ).astype(jnp.float32),
        lax.psum_scatter(
            weight_terms[:, query_cols + key_columns :].astype(jnp.bfloat16),
            "dp",
            scatter_dimension=0,
            tiled=True,
        ).astype(jnp.float32),
    )
    return (attn_out, token_grad, query_grad, key_grad, value_grad)


def solution(mesh):
    placed = (
        P(("dp", "seq"), None),
        P("dp", "seq"),
        P("dp", "seq"),
        P("dp", "seq"),
        P(),
        P(),
        P("dp", None),
        P("dp", "seq"),
    )
    return jax.shard_map(
        local,
        mesh=mesh,
        in_specs=placed,
        out_specs=(
            P(("dp", "seq"), None),
            P(("dp", "seq"), None),
            P("dp", "seq"),
            P("dp", "seq"),
            P("dp", "seq"),
        ),
        check_vma=False,
    )
```

profile of v0, /device:TPU:33, one launch (start us, length us, event | category | flops | bytes accessed | tf_op | source)
XLA Modules:
  0.0 462.9 jit_solution(11136511641203094605)
XLA Ops:
  12.7 14.9 %all_gather.13 = bf16[2688,128]{1,0:T(8,128)(2,1)S(1)} all-gather(bf16[336,128]{1,0:T(8,128)(2,1)} %param.14), channel_id=1, replica_groups=mesh['dp'=8,'seq'=16] {'dp'}, dimensions={0}, use_global_device_ids=true | all-gather | bytes 774144 | tf_op jit(solution)/shard_map/all_gather | solution.py:208
  27.6 13.5 %all_gather.14 = bf16[2688,128]{1,0:T(8,128)(2,1)S(1)} all-gather(bf16[336,128]{1,0:T(8,128)(2,1)S(1)} %copy-done.22), channel_id=1, replica_groups=mesh['dp'=8,'seq'=16] {'dp'}, dimensions={0}, use_global_device_ids=true | all-gather | bytes 774144 | tf_op jit(solution)/shard_map/all_gather | solution.py:209
  43.1 2.9 constant_dynamic-update-slice_fusion.3
  47.9 72.9 %all-gather.5.cloned.1.call-done = bf16[2048,2688]{1,0:T(8,128)(2,1)} async-done(((bf16[128,2688]{1,0:T(8,128)(2,1)}), bf16[2048,2688]{1,0:T(8,128)(2,1)}) %all-gather.5.cloned.1.call-update) | async-done | bytes 11010064 | tf_op jit(solution)/shard_map/all_gather | solution.py:214
  120.8 9.8 %convolution_bitcast_fusion.1 = f32[2048,512]{0,1:T(8,128)S(1)} fusion(bf16[2688,512]{1,0:T(8,128)(2,1)} %constant_dynamic-update-slice_fusion.1, bf16[2048,2688]{1,0:T(8,128)(2,1)} %all-gather.5.cloned.1.call-done), kind=kOutput, calls=%fused_computation.78 | convolution fusion | flops 5637144576 | bytes 17956864 | tf_op jit(solution)/shard_map/dot_general | solution.py:215
  140.7 104.3 %while.36 = (s32[]{:T(128)}, f32[2048,1,2,128]{0,3,2,1:T(8,128)}, f32[2048,1,128]{0,2,1:T(8,128)S(1)}, f32[2048,1,128]{0,2,1:T(8,128)}, bf16[2048,1,128]{2,0,1:T...) while((s32[]{:T(128)}, f32[2048,1,2,128]{0,3,2,1:T(8,128)}, ...), condition=%wide.region_11.12_spmd, body=%wide.region_8.11_spmd.sunk | while | flops 2047016960 | bytes 102170968 | solution.py:189
  142.1 2.7 fusion.125
  144.9 4.1 fusion.126
  157.6 5.1 %fusion.130 = f32[1536,1,128]{0,2,1:T(8,128)S(1)} fusion(f32[2,512]{1,0:T(2,128)S(1)} %get-tuple-element.702, f32[1536,512,2]{1,0,2:T(8,128)} %copy-done, pred[512,1536]{0,1:T(8,128)(4,1)S(1)} %fusion.124, f32[2048,1,128]{0,2,1:T(8,128)} %get-tuple-element.759, s32[]{:T(128)S(6)} %max.25, bf16[2048,1,2,128]{0,3,2,1:T(8,128)(2,1)} %get-tuple-element.778, ...), kind=kOutput, calls=%fused_computation.41.clone.1 | convolution fusion | flops 409141248 | bytes 8917000 | tf_op jit(solution)/shard_map/while/body/eval_jaxpr/hgqk,qhgd->khd/dot_general | solution.py:151
  162.7 4.4 dynamic_update_slice.58
  168.6 2.7 fusion.125
  171.3 4.1 fusion.126
  184.1 5.1 %fusion.130 = f32[1536,1,128]{0,2,1:T(8,128)S(1)} fusion(f32[2,512]{1,0:T(2,128)S(1)} %get-tuple-element.702, f32[1536,512,2]{1,0,2:T(8,128)} %copy-done, pred[512,1536]{0,1:T(8,128)(4,1)S(1)} %fusion.124, f32[2048,1,128]{0,2,1:T(8,128)} %get-tuple-element.759, s32[]{:T(128)S(6)} %max.25, bf16[2048,1,2,128]{0,3,2,1:T(8,128)(2,1)} %get-tuple-element.778, ...), kind=kOutput, calls=%fused_computation.41.clone.1 | convolution fusion | flops 409141248 | bytes 8917000 | tf_op jit(solution)/shard_map/while/body/eval_jaxpr/hgqk,qhgd->khd/dot_general | solution.py:151
  189.1 4.4 dynamic_update_slice.58
  195.0 2.7 fusion.125
  197.8 4.1 fusion.126
  210.5 5.1 %fusion.130 = f32[1536,1,128]{0,2,1:T(8,128)S(1)} fusion(f32[2,512]{1,0:T(2,128)S(1)} %get-tuple-element.702, f32[1536,512,2]{1,0,2:T(8,128)} %copy-done, pred[512,1536]{0,1:T(8,128)(4,1)S(1)} %fusion.124, f32[2048,1,128]{0,2,1:T(8,128)} %get-tuple-element.759, s32[]{:T(128)S(6)} %max.25, bf16[2048,1,2,128]{0,3,2,1:T(8,128)(2,1)} %get-tuple-element.778, ...), kind=kOutput, calls=%fused_computation.41.clone.1 | convolution fusion | flops 409141248 | bytes 8917000 | tf_op jit(solution)/shard_map/while/body/eval_jaxpr/hgqk,qhgd->khd/dot_general | solution.py:151
  215.6 4.4 dynamic_update_slice.58
  221.5 2.7 fusion.125
  224.3 4.1 fusion.126
  236.0 5.0 %fusion.130 = f32[1536,1,128]{0,2,1:T(8,128)S(1)} fusion(f32[2,512]{1,0:T(2,128)S(1)} %get-tuple-element.702, f32[1536,512,2]{1,0,2:T(8,128)} %copy-done, pred[512,1536]{0,1:T(8,128)(4,1)S(1)} %fusion.124, f32[2048,1,128]{0,2,1:T(8,128)} %get-tuple-element.759, s32[]{:T(128)S(6)} %max.25, bf16[2048,1,2,128]{0,3,2,1:T(8,128)(2,1)} %get-tuple-element.778, ...), kind=kOutput, calls=%fused_computation.41.clone.1 | convolution fusion | flops 409141248 | bytes 8917000 | tf_op jit(solution)/shard_map/while/body/eval_jaxpr/hgqk,qhgd->khd/dot_general | solution.py:151
  241.0 3.9 dynamic_update_slice.58
  255.4 6.4 %fusion.65 = bf16[2688,512]{0,1:T(8,128)(2,1)S(1)} fusion(bf16[2048,2688]{1,0:T(8,128)(2,1)S(1)} %bitcast.292, f32[2048,256]{0,1:T(8,128)S(1)} %bitcast.284, f32[2048,128]{0,1:T(8,128)S(1)} %fusion.71, f32[2048,128]{0,1:T(8,128)S(1)} %bitcast.288), kind=kOutput, calls=%fused_computation.77 | convolution fusion | flops 5641666560 | bytes 17956864 | tf_op jit(solution)/shard_map/dot_general | solution.py:237
  269.0 11.4 %convolution_convert_fusion = bf16[2048,2688]{1,0:T(8,128)(2,1)} fusion(bf16[2688,512]{1,0:T(8,128)(2,1)} %constant_dynamic-update-slice_fusion.1, f32[2048,256]{0,1:T(8,128)} %bitcast.285, f32[2048,128]{0,1:T(8,128)S(1)} %fusion.71, f32[2048,128]{0,1:T(8,128)} %bitcast.287), kind=kOutput, calls=%fused_computation.74 | convolution fusion | flops 5645795328 | bytes 17956864 | tf_op jit(solution)/shard_map/dot_general | solution.py:227
  280.5 34.9 %while.35 = (s32[]{:T(128)}, bf16[4,512,256]{2,1,0:T(8,128)(2,1)S(1)}, s32[4]{0:T(128)S(1)}, bf16[2048,1,128]{0,2,1:T(8,128)(2,1)}, s32[2048]{0:T(1024)S(1)}, /*...) while((s32[]{:T(128)}, ...), condition=%wide.region_7.8_spmd, body=%wide.region_5.7_spmd.sunk | while | flops 821167104 | bytes 17350888 | solution.py:142
  285.9 3.1 fusion.117
  294.7 3.1 fusion.117
  303.4 3.1 fusion.117
  312.1 3.1 fusion.117
  315.4 21.0 %all_to_all.19 = bf16[16,128,256]{2,1,0:T(8,128)(2,1)S(1)} all-to-all(bf16[16,128,256]{2,1,0:T(8,128)(2,1)S(1)} %bitcast.289), channel_id=1, replica_groups=mesh['dp'=8,'seq'=16] {'seq'}, dimensions={0} | all-to-all | bytes 2097152 | tf_op jit(solution)/shard_map/all_to_all | solution.py:225
  341.9 17.7 %reduce-scatter.13.cloned.1.call-done = bf16[336,256]{1,0:T(8,128)(2,1)} async-done(((bf16[2688,256]{1,0:T(8,128)(2,1)}), bf16[336,256]{1,0:T(8,128)(2,1)}) %reduce-scatter.13.cloned.1.call-update) | async-done | bytes 172048
  361.6 94.5 %reduce-scatter.11.cloned.1.call-done = bf16[128,2688]{1,0:T(8,128)(2,1)} async-done(((bf16[2048,2688]{1,0:T(8,128)(2,1)}), bf16[128,2688]{1,0:T(8,128)(2,1)}) %reduce-scatter.11.cloned.1.call-update) | async-done | bytes 688144 | tf_op jit(solution)/shard_map/reduce_scatter | solution.py:226
  (222 shorter events, 102.6 us)
Async XLA Ops:
  7.2 20.4 %copy-start.22 = (bf16[336,128]{1,0:T(8,128)(2,1)S(1)}, bf16[336,128]{1,0:T(8,128)(2,1)}, u32[]{:S(2)}) copy-start(bf16[336,128]{1,0:T(8,128)(2,1)} %param.15) | copy-start | bytes 258052
  7.2 35.9 %all-gather.3.cloned.1.call-start = ((), (), s32[]{:S(2)}) async-start(), calls=%async_computation.5 | async-start | bytes 1548288 | tf_op jit(solution)/shard_map/all_gather | solution.py:207
  7.9 112.9 %all-gather.5.cloned.1.call-start = ((), (), s32[]{:S(2)}) async-start(), calls=%async_computation.6 | async-start | bytes 11698176 | tf_op jit(solution)/shard_map/all_gather | solution.py:214
  8.7 329.7 %reduce-scatter.15.cloned.1.call-start = ((), (), s32[]{:S(2)}) async-start(), calls=%async_computation.9 | async-start | bytes 774144
  43.0 90.4 %copy-start.10 = (f32[2048,64]{0,1:T(8,128)}, f32[2048,64]{0,1:T(8,128)S(1)}, u32[]{:S(2)}) copy-start(f32[2048,64]{0,1:T(8,128)S(1)} %get-tuple-element.594) | copy-start | bytes 1572868
  43.0 90.4 %copy-start.12 = (f32[2048,64]{0,1:T(8,128)}, f32[2048,64]{0,1:T(8,128)S(1)}, u32[]{:S(2)}) copy-start(f32[2048,64]{0,1:T(8,128)S(1)} %get-tuple-element.595) | copy-start | bytes 1572868
  130.7 2.8 copy-start.1
  130.8 1.7 copy-start.23
  131.0 1.8 copy-start.18
  131.2 1.6 copy-start.27
  144.9 4.1 copy-start
  149.0 2.0 copy-start.3
  171.3 4.1 copy-start
  175.5 2.0 copy-start.3
  197.8 4.1 copy-start
  201.9 2.0 copy-start.3
  224.2 4.1 copy-start
  228.4 2.0 copy-start.3
  244.9 2.5 copy-start.2
  244.9 2.6 copy-start.11
  244.9 2.6 copy-start.26
  246.4 1.6 copy-start.21
  248.0 1.6 copy-start.5
  248.0 1.8 copy-start.9
  249.8 4.1 slice-start
  250.1 3.9 slice-start.1
  253.0 2.4 slice-start.2
  253.9 7.9 %copy-start.14 = (f32[2048,2,128]{0,2,1:T(8,128)}, f32[2048,2,128]{0,2,1:T(8,128)S(1)}, u32[]{:S(2)}) copy-start(f32[2048,2,128]{0,2,1:T(8,128)S(1)} %add_add_fusion) | copy-start | bytes 6291460
  261.8 1.5 copy-start.13
  264.7 75.5 %reduce-scatter.17.cloned.1.call-start = ((), (), s32[]{:S(2)}) async-start(), calls=%async_computation.10 | async-start | bytes 774144
  265.9 93.7 %reduce-scatter.13.cloned.1.call-start = ((), (), s32[]{:S(2)}) async-start(), calls=%async_computation.8 | async-start | bytes 1548288
  269.0 187.1 %reduce-scatter.11.cloned.1.call-start = ((), (), s32[]{:S(2)}) async-start(), calls=%async_computation.7 | async-start | bytes 11698176 | tf_op jit(solution)/shard_map/reduce_scatter | solution.py:226
  (15 other events, 20.3 us)
Sparse Core Ops, SparseCore 0:
  9.7 25.4 all-gather.2
  37.3 83.4 all-gather.4
  264.8 27.5 reduce-scatter.14
  294.7 30.5 reduce-scatter.16
  327.5 32.0 reduce-scatter.12
  363.5 92.4 reduce-scatter.10
where the time goes:
time: 466 us; the launch traced here: 463 us
  waiting for transfers between devices  187 us (40%)
  matrix products  110 us (24%)
  local copies, waits for them, and re-layouts  69.7 us (15%)
  blocking collectives  49.4 us (11%)
  other arithmetic  29.3 us (6%)
  between operations  14.7 us (3%)
    reduce_scatter x1, waiting for transfers between devices, local(): lax.psum_scatter(lax.dot_general(projection_gradient, joined, (((1,), (1,...  94.5 us
    all_gather x1, waiting for transfers between devices, local(): row_tokens = lax.all_gather(tokens, 'seq', axis=0, tiled=True)  72.9 us
    unnamed x71, local copies, waits for them, and re-layouts  25.3 us
    dot_general x8, matrix products, block_probs(): jnp.einsum('qhgd,khd->hgqk', query_part, key_part, preferred_element_type...  21.7 us
    all_to_all x1, blocking collectives, local(): lax.all_to_all(head_output, 'seq', split_axis=0, concat_axis=1, tiled=True)  21 us
    dot_general x4, matrix products, backward_block(): jnp.einsum('hgqk,qhgd->khd', probs_bf, grad_part, preferred_element_type=...  20.2 us
    unnamed x9, waiting for transfers between devices  19.1 us
    dynamic_update_slice x4, local copies, waits for them, and re-layouts, backward_block(): lax.dynamic_update_slice_in_dim(grad_value, lax.dynamic_slice_in_dim(grad...  17.2 us
  transfers between devices with their start and end apart: 6, of which 3 were waited for; matrix products, arithmetic and copies ran while one was open for 14% of the time, Pallas kernels for 0%

commit v1 on v0

v1 whole, which is shorter than its diff:
```python
import functools
import math

import jax
import jax.numpy as jnp
from jax import lax
from jax.experimental import pallas as pl
from jax.experimental.pallas import tpu as pltpu
from jax.sharding import PartitionSpec as P

HEAD = 128
WINDOW = 1024
BLOCK = 256
score_scale = 168.0 ** (-0.5)
exp_scale = score_scale * math.log2(math.e)
rope_base = 10000.0
norm_eps = 1e-06
NN = (((1,), (0,)), ((), ()))
NT = (((1,), (1,)), ((), ()))


def mm(a, b, dims=NN):
    return lax.dot_general(a, b, dims, preferred_element_type=jnp.float32)


def rope_inputs(length_row, length):
    ends = jnp.cumsum(length_row, dtype=jnp.int32)
    token = jnp.arange(length, dtype=jnp.int32)
    start = jnp.max(jnp.where(token[:, None] >= ends[None, :], ends[None, :], 0), axis=1)
    position = token - start
    half = HEAD // 2
    inverse = rope_base ** (-jnp.arange(half, dtype=jnp.float32) * (2.0 / HEAD))
    angle = position.astype(jnp.float32)[:, None] * inverse[None, :]
    cosine, sine = jnp.cos(angle), jnp.sin(angle)
    return (
        jnp.concatenate([cosine, cosine], axis=1),
        jnp.concatenate([-sine, sine], axis=1),
        ends,
    )


def norm_factor(x):
    return lax.rsqrt(jnp.mean(x * x, axis=-1, keepdims=True) + norm_eps)


def rotate(n, cosine, sine):
    return n * cosine + pltpu.roll(n, HEAD // 2, 1) * sine


def rotate_back(g, cosine, sine):
    return g * cosine + pltpu.roll(g * sine, HEAD // 2, 1)


def norm_back(dn, x, gain):
    factor = norm_factor(x)
    dn = dn * gain
    inner = jnp.sum(x * dn, axis=-1, keepdims=True) * (1.0 / HEAD)
    return factor * dn - x * (factor * factor * factor * inner)


def attention_kernel(
    ends_ref, proj_ref, cot_ref, cos_ref, sin_ref, gq_ref, gk_ref, out_ref, dproj_ref,
    q_s, k_s, kt_s, v_s, vt_s, e_s, eb_s, dk_s, dv_s, acc_s, dot_s, row_s,
):
    length = proj_ref.shape[0]
    blocks = length // BLOCK
    span = WINDOW // BLOCK
    e0, e1, e2 = ends_ref[0], ends_ref[1], ends_ref[2]

    def start_of(t):
        zero = t * 0
        return jnp.maximum(
            jnp.maximum(jnp.where(t >= e0, e0, zero), jnp.where(t >= e1, e1, zero)),
            jnp.where(t >= e2, e2, zero),
        )

    @pl.loop(0, blocks)
    def _(i):
        rows = pl.ds(pl.multiple_of(i * BLOCK, BLOCK), BLOCK)
        cosine, sine = cos_ref[rows, :], sin_ref[rows, :]
        for h in range(2):
            x = proj_ref[rows, h * HEAD : (h + 1) * HEAD]
            n = x * norm_factor(x) * gq_ref[...]
            q_s[i, h * BLOCK : (h + 1) * BLOCK, :] = rotate(n, cosine, sine).astype(jnp.bfloat16)
        x = proj_ref[rows, 2 * HEAD : 3 * HEAD]
        n = x * norm_factor(x) * gk_ref[...]
        key = rotate(n, cosine, sine)
        k_s[i] = key.astype(jnp.bfloat16)
        kt_s[i] = key.T.astype(jnp.bfloat16)
        value = proj_ref[rows, 3 * HEAD : 4 * HEAD]
        v_s[i] = value.astype(jnp.bfloat16)
        vt_s[i] = value.T.astype(jnp.bfloat16)
        dk_s[i] = jnp.zeros((BLOCK, HEAD), jnp.float32)
        dv_s[i] = jnp.zeros((BLOCK, HEAD), jnp.float32)

    @pl.loop(0, blocks)
    def _(i):
        q0 = i * BLOCK
        rows = pl.ds(pl.multiple_of(q0, BLOCK), BLOCK)
        token = q0 + lax.broadcasted_iota(jnp.int32, (1, BLOCK), 1)
        low = jnp.maximum(start_of(token), token - (WINDOW - 1))
        token2 = jnp.concatenate([token, token], axis=1)
        low2 = jnp.concatenate([low, low], axis=1)
        first = jnp.maximum(start_of(q0), q0 - (WINDOW - 1)) // BLOCK
        first = jnp.maximum(first, 0)

        acc_s[...] = jnp.zeros_like(acc_s)
        row_s[...] = jnp.zeros_like(row_s)
        query = q_s[i]

        @pl.loop(first, i + 1)
        def _(j):
            slot = j - i + span
            s = mm(k_s[j], query, NT)
            key_pos = j * BLOCK + lax.broadcasted_iota(jnp.int32, (BLOCK, 2 * BLOCK), 0)
            e = jnp.where((key_pos >= low2) & (key_pos <= token2), jnp.exp2(s * exp_scale), 0.0)
            e_s[slot] = e
            eb = e.astype(jnp.bfloat16)
            eb_s[slot] = eb
            row_s[...] += jnp.sum(e.reshape(BLOCK // 8, 8, 2 * BLOCK), axis=0)
            acc_s[...] += mm(vt_s[j], eb)

        inv = 1.0 / jnp.sum(row_s[...], axis=0, keepdims=True)
        out_t = acc_s[...] * inv
        dot = jnp.concatenate(
            [cot_ref[rows, h * HEAD : (h + 1) * HEAD].astype(jnp.float32).T for h in range(2)], axis=1
        )
        for h in range(2):
            out_ref[rows, h * HEAD : (h + 1) * HEAD] = (
                out_t[:, h * BLOCK : (h + 1) * BLOCK].T.astype(jnp.bfloat16)
            )
        delta = jnp.sum(out_t * dot, axis=0, keepdims=True) * inv
        dot_s[...] = (dot * inv).astype(jnp.bfloat16)
        acc_s[...] = jnp.zeros_like(acc_s)

        @pl.loop(first, i + 1)
        def _(j):
            slot = j - i + span
            dp = mm(v_s[j], dot_s[...])
            ds = (e_s[slot] * (dp - delta)).astype(jnp.bfloat16)
            dv_s[j] += mm(eb_s[slot], dot_s[...], NT)
            dk_s[j] += mm(ds, query)
            acc_s[...] += mm(kt_s[j], ds)

        cosine, sine = cos_ref[rows, :], sin_ref[rows, :]
        for h in range(2):
            g = acc_s[:, h * BLOCK : (h + 1) * BLOCK].T * score_scale
            x = proj_ref[rows, h * HEAD : (h + 1) * HEAD]
            dx = norm_back(rotate_back(g, cosine, sine), x, gq_ref[...])
            dproj_ref[rows, h * HEAD : (h + 1) * HEAD] = dx.astype(jnp.bfloat16)

    @pl.loop(0, blocks)
    def _(i):
        rows = pl.ds(pl.multiple_of(i * BLOCK, BLOCK), BLOCK)
        cosine, sine = cos_ref[rows, :], sin_ref[rows, :]
        x = proj_ref[rows, 2 * HEAD : 3 * HEAD]
        dx = norm_back(rotate_back(dk_s[i] * score_scale, cosine, sine), x, gk_ref[...])
        dproj_ref[rows, 2 * HEAD : 3 * HEAD] = dx.astype(jnp.bfloat16)
        dproj_ref[rows, 3 * HEAD : 4 * HEAD] = dv_s[i].astype(jnp.bfloat16)


def attention(ends, proj, cot, cosine, sine, gain_q, gain_k):
    length = proj.shape[0]
    blocks = length // BLOCK
    slots = WINDOW // BLOCK + 1
    vmem = pl.BlockSpec(memory_space=pltpu.VMEM)
    bf, f32 = jnp.bfloat16, jnp.float32
    return pl.pallas_call(
        attention_kernel,
        out_shape=(
            jax.ShapeDtypeStruct((length, 2 * HEAD), bf),
            jax.ShapeDtypeStruct((length, 4 * HEAD), bf),
        ),
        in_specs=[pl.BlockSpec(memory_space=pltpu.SMEM)] + [vmem] * 6,
        out_specs=(vmem, vmem),
        scratch_shapes=[
            pltpu.VMEM((blocks, 2 * BLOCK, HEAD), bf),
            pltpu.VMEM((blocks, BLOCK, HEAD), bf),
            pltpu.VMEM((blocks, HEAD, BLOCK), bf),
            pltpu.VMEM((blocks, BLOCK, HEAD), bf),
            pltpu.VMEM((blocks, HEAD, BLOCK), bf),
            pltpu.VMEM((slots, BLOCK, 2 * BLOCK), f32),
            pltpu.VMEM((slots, BLOCK, 2 * BLOCK), bf),
            pltpu.VMEM((blocks, BLOCK, HEAD), f32),
            pltpu.VMEM((blocks, BLOCK, HEAD), f32),
            pltpu.VMEM((HEAD, 2 * BLOCK), f32),
            pltpu.VMEM((HEAD, 2 * BLOCK), bf),
            pltpu.VMEM((8, 2 * BLOCK), f32),
        ],
        compiler_params=pltpu.CompilerParams(vmem_limit_bytes=48 * 1024 * 1024),
        name="attention",
    )(ends, proj, cot, cosine, sine, gain_q.reshape(1, HEAD), gain_k.reshape(1, HEAD))


def local(
    tokens, q_weight, key_projection, value_projection, query_norm_gain, key_norm_gain, doc_lengths, out_cot
):
    joined = jnp.concatenate([q_weight, key_projection, value_projection], axis=1)
    joined = lax.all_gather(joined, "dp", axis=0, tiled=True)
    row_tokens = lax.all_gather(tokens, "seq", axis=0, tiled=True)
    cosine, sine, ends = rope_inputs(doc_lengths[0], row_tokens.shape[0])
    proj = jnp.dot(row_tokens, joined, preferred_element_type=jnp.float32)
    head_output, dproj = attention(ends, proj, out_cot, cosine, sine, query_norm_gain, key_norm_gain)
    token_grad = lax.psum_scatter(
        lax.dot_general(dproj, joined, NT, preferred_element_type=jnp.float32).astype(jnp.bfloat16),
        "seq",
        scatter_dimension=0,
        tiled=True,
    )
    weight_terms = lax.dot_general(
        row_tokens, dproj, (((0,), (0,)), ((), ())), preferred_element_type=jnp.float32
    ).astype(jnp.bfloat16)
    grads = lax.psum_scatter(weight_terms, "dp", scatter_dimension=0, tiled=True).astype(jnp.float32)
    attn_out = lax.all_to_all(head_output, "seq", split_axis=0, concat_axis=1, tiled=True)
    qc = q_weight.shape[1]
    kc = key_projection.shape[1]
    return (attn_out, token_grad, grads[:, :qc], grads[:, qc : qc + kc], grads[:, qc + kc :])


def solution(mesh):
    placed = (
        P(("dp", "seq"), None),
        P("dp", "seq"),
        P("dp", "seq"),
        P("dp", "seq"),
        P(),
        P(),
        P("dp", None),
        P("dp", "seq"),
    )
    return jax.shard_map(
        local,
        mesh=mesh,
        in_specs=placed,
        out_specs=(
            P(("dp", "seq"), None),
            P(("dp", "seq"), None),
            P("dp", "seq"),
            P("dp", "seq"),
            P("dp", "seq"),
        ),
        check_vma=False,
    )
```

time: 466 us -> 323 us (0.69)
  matrix products: 110 us -> 30.7 us
  local copies, waits for them, and re-layouts: 69.7 us -> 11.9 us
  Pallas kernels: 0 us -> 33.3 us
  blocking collectives: 49.4 us -> 17.8 us
  other arithmetic: 29.3 us -> 7.04 us
  waiting for transfers between devices: 187 us -> 205 us
    dot_general x31 -> x3, matrix products: 110 us -> 30.7 us  [the longest x1 11.4 us: local(): proj = jnp.dot(row_tokens, joined, preferred_element_type=jnp.float32)]
    pallas_call x0 -> x1, Pallas kernels: none -> 33.3 us  [attention(): pl.pallas_call(attention_kernel, out_shape=(jax.ShapeDtypeStruct((length,...]
    all_gather x2 -> x0, blocking collectives: 28.5 us -> none  [the longest x1 14.9 us: local(): lax.all_gather(key_projection, 'dp', axis=0, tiled=True)]
    dynamic_update_slice x16 -> x0, local copies, waits for them, and re-layouts: 26.2 us -> none  [the longest x4 17.2 us: backward_block(): lax.dynamic_update_slice_in_dim(grad_value, lax.dynamic_slice_in_dim(grad...]
    all_gather x1, waiting for transfers between devices: 0.02 us -> 23.2 us  [local(): joined = lax.all_gather(joined, 'dp', axis=0, tiled=True)]
    unnamed x9 -> x5, waiting for transfers between devices: 19.1 us -> 3.87 us
    unnamed x71 -> x15, local copies, waits for them, and re-layouts: 25.3 us -> 10.8 us
    all_gather x1, waiting for transfers between devices: 72.9 us -> 85.2 us  [local(): row_tokens = lax.all_gather(tokens, 'seq', axis=0, tiled=True)]
  transfers between devices with their start and end apart: 6 -> 4, of which waited for: 3 -> 4; matrix products, arithmetic and copies ran while one was open for 14% -> 6% of each run, Pallas kernels for 0% -> 0%
where the time goes in v1:
time: 323 us; the launch traced here: 320 us
  waiting for transfers between devices  205 us (63%)
  Pallas kernels  33.3 us (10%)
  matrix products  30.7 us (10%)
  blocking collectives  17.8 us (6%)
  between operations  13.8 us (4%)
  local copies, waits for them, and re-layouts  11.9 us (4%)
  other arithmetic  7.04 us (2%)
    reduce_scatter x1, waiting for transfers between devices, local(): lax.psum_scatter(lax.dot_general(dproj, joined, NT, preferred_element_typ...  93 us
    all_gather x1, waiting for transfers between devices, local(): row_tokens = lax.all_gather(tokens, 'seq', axis=0, tiled=True)  85.2 us
    pallas_call x1, Pallas kernels, attention(): pl.pallas_call(attention_kernel, out_shape=(jax.ShapeDtypeStruct((length,...  33.3 us
    all_gather x1, waiting for transfers between devices, local(): joined = lax.all_gather(joined, 'dp', axis=0, tiled=True)  23.2 us
    all_to_all x1, blocking collectives, local(): lax.all_to_all(head_output, 'seq', split_axis=0, concat_axis=1, tiled=True)  17.8 us
    dot_general x1, matrix products, local(): proj = jnp.dot(row_tokens, joined, preferred_element_type=jnp.float32)  11.4 us
    unnamed x15, local copies, waits for them, and re-layouts  10.8 us
    dot_general x1, matrix products, local(): lax.dot_general(dproj, joined, NT, preferred_element_type=jnp.float32)  10.6 us
  transfers between devices with their start and end apart: 4, of which 4 were waited for; matrix products, arithmetic and copies ran while one was open for 6% of the time, Pallas kernels for 0%

profile of v1, /device:TPU:33, one launch (start us, length us, event | category | flops | bytes accessed | tf_op | source)
XLA Modules:
  0.0 320.3 jit_solution(15311632353388434726)
XLA Ops:
  7.2 0.0 all-gather.3.cloned.1.call-start
  7.2 1.8 pad_maximum_fusion.2
  9.0 0.0 all-gather.3.cloned.1.call-update
  9.0 0.0 all-gather.5.cloned.1.call-start
  9.0 0.7 all-gather.5.cloned.1.call-update
  9.8 0.0 reduce-scatter.7.cloned.1.call-start
  9.8 0.8 reduce-window.8
  10.6 0.1 select_reduce_fusion
  10.8 3.7 %fusion.1 = (f32[2048,64]{1,0:T(8,128)S(1)}, f32[2048,64]{1,0:T(8,128)S(1)}, f32[2048,64]{1,0:T(8,128)S(1)}) fusion(f32[64]{0:T(128)S(1)} %multiply_power_fusion, f32[2048]{0:T(1024)S(1)} %subtract_convert_fusion), kind=kLoop, calls=%fused_computation.9 | loop fusion | flops 262144 | bytes 1581312 | tf_op jit(solution)/shard_map/neg | solution.py:37
  14.5 0.6 pad_maximum_fusion
  15.1 0.0 copy-start.1
  15.1 0.0 copy-start.2
  15.1 23.2 %all-gather.3.cloned.1.call-done = bf16[2688,512]{1,0:T(8,128)(2,1)} async-done(((bf16[336,512]{1,0:T(8,128)(2,1)}), bf16[2688,512]{1,0:T(8,128)(2,1)}) %all-gather.3.cloned.1.call-update) | async-done | bytes 2752528 | tf_op jit(solution)/shard_map/all_gather | solution.py:199
  38.4 85.2 %all-gather.5.cloned.1.call-done = bf16[2048,2688]{1,0:T(8,128)(2,1)} async-done(((bf16[128,2688]{1,0:T(8,128)(2,1)}), bf16[2048,2688]{1,0:T(8,128)(2,1)}) %all-gather.5.cloned.1.call-update) | async-done | bytes 11010064 | tf_op jit(solution)/shard_map/all_gather | solution.py:200
  123.5 11.4 %convolution_bitcast_fusion.proj_ref = f32[2048,512]{1,0:T(8,128)} fusion(bf16[2048,2688]{1,0:T(8,128)(2,1)} %all-gather.5.cloned.1.call-done, bf16[2688,512]{1,0:T(8,128)(2,1)} %all-gather.3.cloned.1.call-done), kind=kOutput, calls=%fused_computation.3 | convolution fusion | flops 5637144576 | bytes 17956864 | tf_op jit(solution)/shard_map/dot_general | solution.py:202
  134.9 1.2 copy-done
  136.1 33.3 %attention.1 = (bf16[2048,256]{1,0:T(8,128)(2,1)S(1)}, bf16[2048,512]{1,0:T(8,128)(2,1)}) custom-call(s32[4]{0:T(128)S(1)} %bitcast.21, f32[2048,512]{1,0:T(8,128)} %convolution_bitcast_fusion.proj_ref, bf16[2048,256]{1,0:T(8,128)(2,1)S(1)} %copy-done, f32[2048,128]{1,0:T(8,128)S(1)} %get-tuple-element.29.cos_ref, ...), custom_call_target="tpu_custom_call" | custom-call | tf_op jit(solution)/shard_map/attention/pallas_call | solution.py:168
  169.5 8.7 %fusion = bf16[2688,512]{0,1:T(8,128)(2,1)} fusion(bf16[2048,512]{1,0:T(8,128)(2,1)} %get-tuple-element.8, bf16[2048,2688]{1,0:T(8,128)(2,1)S(1)} %copy-done.3), kind=kOutput, calls=%fused_computation.2 | convolution fusion | flops 5638520832 | bytes 15859712 | tf_op jit(solution)/shard_map/dot_general | solution.py:210
  178.2 4.6 %copy.29 = bf16[2688,512]{1,0:T(8,128)(2,1)} copy(bf16[2688,512]{0,1:T(8,128)(2,1)} %fusion) | data formatting | bytes 5505024
  182.8 0.0 reduce-scatter.7.cloned.1.call-update
  182.8 0.2 reduce-scatter.5.cloned.1.call-start
  183.0 1.3 copy-done.4
  184.4 10.6 %convolution_convert_fusion = bf16[2048,2688]{1,0:T(8,128)(2,1)} fusion(bf16[2048,512]{1,0:T(8,128)(2,1)S(1)} %copy-done.4, bf16[2688,512]{1,0:T(8,128)(2,1)} %all-gather.3.cloned.1.call-done), kind=kOutput, calls=%fused_computation | convolution fusion | flops 5642649600 | bytes 15859712 | tf_op jit(solution)/shard_map/dot_general | solution.py:205
  195.0 0.0 reduce-scatter.5.cloned.1.call-update
  195.0 17.8 %all_to_all.19 = bf16[16,128,256]{2,1,0:T(8,128)(2,1)S(1)} all-to-all(bf16[16,128,256]{2,1,0:T(8,128)(2,1)S(1)} %bitcast.19), channel_id=1, replica_groups=mesh['dp'=8,'seq'=16] {'seq'}, dimensions={0} | all-to-all | bytes 2097152 | tf_op jit(solution)/shard_map/all_to_all | solution.py:214
  212.8 1.1 copy.31
  213.9 3.1 reduce-scatter.7.cloned.1.call-done
  217.0 1.2 copy.30
  218.3 0.9 copy.25
  219.2 0.8 copy.27
  220.0 0.8 copy.26
  220.8 93.0 %reduce-scatter.5.cloned.1.call-done = bf16[128,2688]{1,0:T(8,128)(2,1)} async-done(((bf16[2048,2688]{1,0:T(8,128)(2,1)}), bf16[128,2688]{1,0:T(8,128)(2,1)}) %reduce-scatter.5.cloned.1.call-update) | async-done | bytes 688144 | tf_op jit(solution)/shard_map/reduce_scatter | solution.py:204
  (10 shorter events, 0.1 us)
Async XLA Ops:
  7.2 31.2 %all-gather.3.cloned.1.call-start = ((), (), s32[]{:S(2)}) async-start(), calls=%async_computation.3 | async-start | bytes 3096576 | tf_op jit(solution)/shard_map/all_gather | solution.py:199
  9.0 114.5 %all-gather.5.cloned.1.call-start = ((), (), s32[]{:S(2)}) async-start(), calls=%async_computation.4 | async-start | bytes 11698176 | tf_op jit(solution)/shard_map/all_gather | solution.py:200
  9.8 207.3 %reduce-scatter.7.cloned.1.call-start = ((), (), s32[]{:S(2)}) async-start(), calls=%async_computation.6 | async-start | bytes 3096576
  15.1 119.8 %copy-start.1 = (f32[128]{0:T(128)S(1)}, f32[128]{0:T(128)}, u32[]{:S(2)}) copy-start(f32[128]{0:T(128)} %param.12) | copy-start | bytes 1540
  15.1 119.8 %copy-start.2 = (f32[128]{0:T(128)S(1)}, f32[128]{0:T(128)}, u32[]{:S(2)}) copy-start(f32[128]{0:T(128)} %param.13) | copy-start | bytes 1540
  123.5 46.0 %copy-start.3 = (bf16[2048,2688]{1,0:T(8,128)(2,1)S(1)}, bf16[2048,2688]{1,0:T(8,128)(2,1)}, u32[]{:S(2)}) copy-start(bf16[2048,2688]{1,0:T(8,128)(2,1)} %all-gather.5.cloned.1.call-done) | copy-start | bytes 33030148
  134.9 1.2 copy-start
  182.8 1.6 copy-start.4
  182.8 131.0 %reduce-scatter.5.cloned.1.call-start = ((), (), s32[]{:S(2)}) async-start(), calls=%async_computation.5 | async-start | bytes 11698176 | tf_op jit(solution)/shard_map/reduce_scatter | solution.py:204
Sparse Core Ops, SparseCore 0:
  10.2 28.0 all-gather.2
  40.5 82.9 all-gather.4
  182.9 34.0 reduce-scatter.6
  220.9 92.8 reduce-scatter.4

commit v2 on v1

--- a/solution.py
+++ b/solution.py
@@ -23,11 +23,8 @@
     return lax.dot_general(a, b, dims, preferred_element_type=jnp.float32)
 
 
-def rope_inputs(length_row, length):
-    ends = jnp.cumsum(length_row, dtype=jnp.int32)
-    token = jnp.arange(length, dtype=jnp.int32)
-    start = jnp.max(jnp.where(token[:, None] >= ends[None, :], ends[None, :], 0), axis=1)
-    position = token - start
+def rope_inputs(length):
+    position = jnp.arange(length, dtype=jnp.int32)
     half = HEAD // 2
     inverse = rope_base ** (-jnp.arange(half, dtype=jnp.float32) * (2.0 / HEAD))
     angle = position.astype(jnp.float32)[:, None] * inverse[None, :]
@@ -35,7 +32,6 @@
     return (
         jnp.concatenate([cosine, cosine], axis=1),
         jnp.concatenate([-sine, sine], axis=1),
-        ends,
     )
 
 
@@ -59,13 +55,18 @@
 
 
 def attention_kernel(
-    ends_ref, proj_ref, cot_ref, cos_ref, sin_ref, gq_ref, gk_ref, out_ref, dproj_ref,
-    q_s, k_s, kt_s, v_s, vt_s, e_s, eb_s, dk_s, dv_s, acc_s, dot_s, row_s,
+    docs_ref, docs2_ref, proj_ref, cot_own, cot_got, cos_ref, sin_ref, gq_ref, gk_ref, out_ref, dproj_ref,
+    cot_ref, cot_sem, q_s, k_s, kt_s, v_s, vt_s, e_s, eb_s, dk_s, dv_s, acc_s, dot_s, row_s,
 ):
     length = proj_ref.shape[0]
     blocks = length // BLOCK
     span = WINDOW // BLOCK
-    e0, e1, e2 = ends_ref[0], ends_ref[1], ends_ref[2]
+    same = docs_ref[0, 4] == 1
+    pl.when(same)(lambda: pltpu.make_async_copy(cot_own, cot_ref, cot_sem).start())
+    pl.when(jnp.logical_not(same))(lambda: pltpu.make_async_copy(cot_got, cot_ref, cot_sem).start())
+    e0, e1, e2 = [jnp.where(same, docs_ref[0, k], docs2_ref[0, k]) for k in range(3)]
+    e1 = e0 + e1
+    e2 = e1 + e2
 
     def start_of(t):
         zero = t * 0
@@ -93,6 +94,8 @@
         dk_s[i] = jnp.zeros((BLOCK, HEAD), jnp.float32)
         dv_s[i] = jnp.zeros((BLOCK, HEAD), jnp.float32)
 
+    pltpu.make_async_copy(cot_own, cot_ref, cot_sem).wait()
+
     @pl.loop(0, blocks)
     def _(i):
         q0 = i * BLOCK
@@ -159,7 +162,7 @@
         dproj_ref[rows, 3 * HEAD : 4 * HEAD] = dv_s[i].astype(jnp.bfloat16)
 
 
-def attention(ends, proj, cot, cosine, sine, gain_q, gain_k):
+def attention(docs, docs2, proj, cot, cot2, cosine, sine, gain_q, gain_k):
     length = proj.shape[0]
     blocks = length // BLOCK
     slots = WINDOW // BLOCK + 1
@@ -171,9 +174,13 @@
             jax.ShapeDtypeStruct((length, 2 * HEAD), bf),
             jax.ShapeDtypeStruct((length, 4 * HEAD), bf),
         ),
-        in_specs=[pl.BlockSpec(memory_space=pltpu.SMEM)] + [vmem] * 6,
+        in_specs=[pl.BlockSpec(memory_space=pltpu.SMEM)] * 2
+        + [vmem, pl.BlockSpec(memory_space=pl.ANY), pl.BlockSpec(memory_space=pl.ANY)]
+        + [vmem] * 4,
         out_specs=(vmem, vmem),
         scratch_shapes=[
+            pltpu.VMEM((length, 2 * HEAD), bf),
+            pltpu.SemaphoreType.DMA(()),
             pltpu.VMEM((blocks, 2 * BLOCK, HEAD), bf),
             pltpu.VMEM((blocks, BLOCK, HEAD), bf),
             pltpu.VMEM((blocks, HEAD, BLOCK), bf),
@@ -189,32 +196,436 @@
         ],
         compiler_params=pltpu.CompilerParams(vmem_limit_bytes=48 * 1024 * 1024),
         name="attention",
-    )(ends, proj, cot, cosine, sine, gain_q.reshape(1, HEAD), gain_k.reshape(1, HEAD))
+    )(docs, docs2, proj, cot, cot2, cosine, sine, gain_q.reshape(1, HEAD), gain_k.reshape(1, HEAD))
+
+
+MESH = pl.DeviceIdType.MESH
+KH = 1408
+HALF_ROWS = 64
+
+
+class Place:
+    def __init__(self):
+        d, s = lax.axis_index("dp"), lax.axis_index("seq")
+        self.z, self.c = d // 2, d % 2
+        self.y, self.x = s // 4, s % 4
+        self.t = self.x // 2
+        self.xp = 3 - self.x
+        self.xs = self.x + 1 - 2 * (self.x % 2)
+        self.xsp = 3 - self.xs
+        self.up_y, self.down_y, self.far_y = (self.y + 1) % 4, (self.y + 3) % 4, (self.y + 2) % 4
+        self.same = self.c == self.t
+        self.beside = self.at(x=self.xs)
+        self.up, self.down = self.at(y=self.up_y), self.at(y=self.down_y)
+        self.sibling = self.at(c=1 - self.c)
+
+    def at(self, z=None, c=None, y=None, x=None):
+        z = self.z if z is None else z
+        c = self.c if c is None else c
+        y = self.y if y is None else y
+        x = self.x if x is None else x
+        return (z * 2 + c, y * 4 + x)
+
+
+class Sends:
+    def __init__(self, sems):
+        self.sems, self.count, self.open = sems, 0, []
+
+    def sem(self):
+        self.count += 1
+        return self.sems.at[self.count - 1]
+
+    def send(self, src, dst, recv, device, when=None):
+        copy = pltpu.make_async_remote_copy(
+            src_ref=src, dst_ref=dst, send_sem=self.sem(), recv_sem=recv,
+            device_id=device, device_id_type=MESH,
+        )
+        if when is None:
+            copy.start()
+        else:
+            pl.when(when)(copy.start)
+        self.open.append((copy, when))
+
+    def finish(self):
+        for copy, when in self.open:
+            if when is None:
+                copy.wait_send()
+            else:
+                pl.when(when)(copy.wait_send)
+
+
+def arrive(dst, sem):
+    pltpu.make_async_copy(dst, dst, sem).wait()
+
+
+def gather_kernel(
+    tok2, wj, cot, docs, proj_out, tok_out, w_out, cot_out, docs_out,
+    tok, w, wx, other, sib, send_s, p_s, q_s, first_s, w_s, misc_s, sib_s, local_s,
+):
+    me = Place()
+    z, c, y, x, t, same = me.z, me.c, me.y, me.x, me.t, me.same
+    sends = Sends(send_s)
+    width = 4 * HEAD
+    part = {"p": (pl.ds(0, HALF_ROWS), p_s), "q": (pl.ds(HALF_ROWS, HALF_ROWS), q_s)}
+    piece_rows = wj.shape[0]
+
+    def forward(name, slot, device):
+        rows, sems = part[name]
+        ref = tok.at[slot, rows, :]
+        sends.send(ref, ref, sems.at[slot], device)
+
+    def landed(name, slot):
+        rows, sems = part[name]
+        arrive(tok.at[slot, rows, :], sems.at[slot])
+
+    own, pair = y * 4 + x, y * 4 + me.xp
+    target_x = jnp.where(same, x, me.xp)
+    first = first_s.at[jnp.where(same, 0, 1)]
+    for k in range(2):
+        local = same & (c == k)
+        sends.send(tok2.at[k], tok.at[own], first, me.at(c=k, x=target_x), when=jnp.logical_not(local))
+
+        @pl.when(local)
+        def _():
+            pltpu.make_async_copy(tok2.at[k], tok.at[own], first_s.at[0]).start()
+
+    sends.send(wj, wx, misc_s.at[0], me.at(x=me.xp))
+    sends.send(docs, docs_out, misc_s.at[2], me.sibling)
+
+    target_c = z // 2
+    piece = (z % 2) * 2 + c
+
+    def spread(src, g):
+        rows = pl.ds(pl.multiple_of(piece * piece_rows, 16), piece_rows)
+        dst = w.at[rows, pl.ds(pl.multiple_of(g * width, width), width)]
+        sem = w_s.at[piece * 2 + g]
+        here = target_c == c
+        for k in (1, 3, 2):
+            sends.send(src, dst, sem, me.at(z=(z + k) % 4, c=target_c))
+        sends.send(src, dst, sem, me.sibling, when=jnp.logical_not(here))
+
+        @pl.when(here)
+        def _():
+            pltpu.make_async_copy(src, dst, sem).start()
+
+    w[pl.ds(4 * piece_rows, KH - 4 * piece_rows), :] = jnp.zeros((KH - 4 * piece_rows, 2 * width), jnp.bfloat16)
+    for slot, sem in ((own, 0), (pair, 1)):
+        arrive(tok.at[slot], first_s.at[sem])
+        forward("q", slot, me.up)
+        forward("q", slot, me.down)
+        forward("p", slot, me.beside)
+        forward("p", slot, me.up)
+        forward("p", slot, me.down)
+        forward("q", slot, me.beside)
+        if sem == 0:
+            spread(wj, t)
+    arrive(wx, misc_s.at[0])
+    spread(wx, 1 - t)
+    swap = jnp.logical_not(same)
+    sends.send(cot, cot_out, misc_s.at[1], me.at(c=1 - c, x=me.xp), when=swap)
+
+    for column in (me.xs, me.xsp):
+        slot = y * 4 + column
+        landed("p", slot)
+        forward("p", slot, me.up)
+        forward("p", slot, me.down)
+    below, above, far = me.down_y * 4, me.up_y * 4, me.far_y * 4
+    landed("q", below + x)
+    forward("q", below + x, me.up)
+    forward("q", below + x, me.beside)
+    landed("q", above + me.xp)
+    forward("q", above + me.xp, me.down)
+    forward("q", above + me.xp, me.beside)
+    landed("q", below + me.xp)
+    forward("q", below + me.xp, me.beside)
+    landed("q", above + x)
+    forward("q", above + x, me.beside)
+    for column in (x, me.xp):
+        landed("p", below + column)
+        forward("p", below + column, me.up)
+    for column in (me.xs, me.xsp):
+        landed("p", above + column)
+        forward("p", above + column, me.down)
+    for column in (x, me.xp):
+        landed("q", far + column)
+        forward("q", far + column, me.beside)
+
+    for i in range(4):
+        for g in range(2):
+            arrive(
+                w.at[pl.ds(i * piece_rows, piece_rows), pl.ds(g * width, width)], w_s.at[i * 2 + g]
+            )
+    pltpu.make_async_copy(w, w_out, local_s.at[4]).start()
+
+    beside = (me.xs, me.xsp)
+    here = (x, me.xp)
+    plan = (
+        (me.y, (), beside),
+        (me.down_y, beside, beside),
+        (me.up_y, here, beside),
+        (me.far_y, here + beside, beside),
+    )
+    for n, (row, need_p, need_q) in enumerate(plan):
+        for column in need_p:
+            landed("p", row * 4 + column)
+        for column in need_q:
+            landed("q", row * 4 + column)
+        slots = pl.ds(pl.multiple_of(row * 4, 4), 4)
+        rows = pl.ds(pl.multiple_of(row * 512, 512), 512)
+        pltpu.make_async_copy(tok.at[slots], tok_out.at[slots], local_s.at[n]).start()
+        block = tok[slots].reshape(512, KH)
+        other[rows, :] = mm(block, w[:, pl.ds(pl.multiple_of((1 - c) * width, width), width)])
+        sends.send(other.at[rows, :], sib.at[rows, :], sib_s.at[n], me.sibling)
+        proj_out[rows, :] = mm(block, w[:, pl.ds(pl.multiple_of(c * width, width), width)])
+    for n, (row, _, _) in enumerate(plan):
+        rows = pl.ds(pl.multiple_of(row * 512, 512), 512)
+        arrive(sib.at[rows, :], sib_s.at[n])
+        proj_out[rows, :] += sib[rows, :]
+        slots = pl.ds(pl.multiple_of(row * 4, 4), 4)
+        pltpu.make_async_copy(tok.at[slots], tok_out.at[slots], local_s.at[n]).wait()
+    pltpu.make_async_copy(w, w_out, local_s.at[4]).wait()
+    arrive(docs_out, misc_s.at[2])
+    pl.when(swap)(lambda: arrive(cot_out, misc_s.at[1]))
+    sends.finish()
+
+
+def gather(tok2, wj, cot, docs):
+    f32, bf = jnp.float32, jnp.bfloat16
+    anywhere = pl.BlockSpec(memory_space=pl.ANY)
+    dma = pltpu.SemaphoreType.DMA
+    length = cot.shape[0]
+    return pl.pallas_call(
+        gather_kernel,
+        out_shape=(
+            jax.ShapeDtypeStruct((length, 4 * HEAD), f32),
+            jax.ShapeDtypeStruct((16, 128, KH), bf),
+            jax.ShapeDtypeStruct((KH, 8 * HEAD), bf),
+            jax.ShapeDtypeStruct(cot.shape, bf),
+            jax.ShapeDtypeStruct(docs.shape, docs.dtype),
+        ),
+        in_specs=[anywhere] * 4,
+        out_specs=(pl.BlockSpec(memory_space=pltpu.VMEM),) + (anywhere,) * 4,
+        scratch_shapes=[
+            pltpu.VMEM((16, 128, KH), bf),
+            pltpu.VMEM((KH, 8 * HEAD), bf),
+            pltpu.VMEM(wj.shape, bf),
+            pltpu.VMEM((length, 4 * HEAD), f32),
+            pltpu.VMEM((length, 4 * HEAD), f32),
+            dma((60,)), dma((16,)), dma((16,)), dma((2,)), dma((8,)), dma((3,)), dma((4,)), dma((5,)),
+        ],
+        compiler_params=pltpu.CompilerParams(
+            has_side_effects=True, vmem_limit_bytes=56 * 1024 * 1024
+        ),
+        name="gather",
+    )(tok2, wj, cot, docs)
+
+
+def scatter_kernel(
+    attn, dproj, tok_in, w_in, attn_out, grad_out, gq_out, gk_out, gv_out,
+    tok, w, dpj, terms, dw, rqx, rp1, rp2, rpx, rq1, rq2, rw,
+    send_s, attn_s, dp_s, local_s, qx_s, p1_s, p2_s, px_s, q1_s, q2_s, rw_s, g_s,
+):
+    me = Place()
+    z, c, y, x, t, same = me.z, me.c, me.y, me.x, me.t, me.same
+    sends = Sends(send_s)
+    width = 4 * HEAD
+    p_rows, q_rows = pl.ds(0, HALF_ROWS), pl.ds(HALF_ROWS, HALF_ROWS)
+    order = (me.far_y, me.up_y, me.down_y, y)
+    mine = pl.ds(pl.multiple_of(c * width, width), width)
+    piece_rows = gq_out.shape[0]
+
+    pltpu.make_async_copy(w_in, w, local_s.at[4]).start()
+    for n, row in enumerate(order):
+        rows = pl.ds(pl.multiple_of(row * 512, 512), 512)
+        pltpu.make_async_copy(dproj.at[rows, :], dpj.at[rows, mine], local_s.at[n]).start()
+        sends.send(dproj.at[rows, :], dpj.at[rows, mine], dp_s.at[n], me.sibling)
+    pltpu.make_async_copy(tok_in, tok, local_s.at[5]).start()
+
+    def add(dst, *sources):
+        total = dst[...].astype(jnp.float32)
+        for source in sources:
+            total = total + source[...].astype(jnp.float32)
+        dst[...] = total.astype(jnp.bfloat16)
+
+    def compute(n):
+        row = order[n]
+        rows = pl.ds(pl.multiple_of(row * 512, 512), 512)
+        arrive(dpj.at[rows, pl.ds(0, width)], local_s.at[n])
+        arrive(dpj.at[rows, pl.ds(0, width)], dp_s.at[n])
+        if n == 0:
+            arrive(w, local_s.at[4])
+        slots = pl.ds(pl.multiple_of(row * 4, 4), 4)
+        term = mm(dpj[rows, :], w[...], NT).astype(jnp.bfloat16)
+        terms[slots] = term.reshape(4, 128, KH)
+        for k, column in enumerate((me.xs, me.xsp)):
+            sends.send(terms.at[row * 4 + column, q_rows, :], rqx.at[n, k], qx_s.at[n, k], me.beside)
+
+    far, up, down, own = me.far_y * 4, me.up_y * 4, me.down_y * 4, y * 4
+    compute(0)
+    sends.send(terms.at[pl.ds(far, 2), p_rows, :], rp1.at[0], p1_s.at[0], me.up)
+    sends.send(terms.at[pl.ds(far + 2, 2), p_rows, :], rp1.at[1], p1_s.at[1], me.down)
+    compute(1)
+    compute(2)
+    compute(3)
+    arrive(rp1.at[0], p1_s.at[0])
+    add(terms.at[pl.ds(up, 2), p_rows, :], rp1.at[0])
+    sends.send(terms.at[pl.ds(up, 4), p_rows, :], rp2.at[0], p2_s.at[0], me.up)
+    arrive(rp1.at[1], p1_s.at[1])
+    add(terms.at[pl.ds(down + 2, 2), p_rows, :], rp1.at[1])
+    sends.send(terms.at[pl.ds(down, 4), p_rows, :], rp2.at[1], p2_s.at[1], me.down)
+
+    group = y * 4 + jnp.where(same, x, me.xp)
+    columns = pl.ds(pl.multiple_of(group * 2 * HEAD, 2 * HEAD), 2 * HEAD)
+    for dy in range(4):
+        for dx in range(4):
+            to_y, to_x = (y + dy) % 4, (x + dx) % 4
+            rows = pl.ds(pl.multiple_of((to_y * 4 + to_x) * 128, 128), 128)
+            src, dst = attn.at[rows, :], attn_out.at[:, columns]
+            if dy == 0 and dx == 0:
+                sends.send(src, dst, attn_s.at[group], me.sibling, when=jnp.logical_not(same))
+
+                @pl.when(same)
+                def _():
+                    pltpu.make_async_copy(src, dst, attn_s.at[group]).start()
+            else:
+                sends.send(src, dst, attn_s.at[group], me.at(c=t, y=to_y, x=to_x))
+
+    def weight_terms(i):
+        if i == 0:
+            arrive(tok, local_s.at[5])
+        low, high = i * 384, min(KH, i * 384 + 384)
+        cut = min(high, 4 * piece_rows)
+        left = tok[:, :, low:high].reshape(16 * 128, high - low)
+        term = mm(left, dpj[...], (((0,), (0,)), ((), ())))
+        dw[low:cut, :] = term[: cut - low].astype(jnp.bfloat16)
+        for g in range(2):
+            src = dw.at[pl.ds(i * piece_rows, piece_rows), pl.ds(g * width, width)]
+            dst, sem = rw.at[z * 2 + t], rw_s.at[z * 2 + t]
+            to_z, to_c = 2 * c + i // 2, i % 2
+            stays = (to_z == z) & (c == to_c) & (t == g)
+            sends.send(
+                src, dst, sem, me.at(z=to_z, c=to_c, x=jnp.where(t == g, x, me.xp)),
+                when=jnp.logical_not(stays),
+            )
+
+            @pl.when(stays)
+            def _():
+                pltpu.make_async_copy(src, dst, sem).start()
+
+    def exchanged(n):
+        for k, column in enumerate((x, me.xp)):
+            arrive(rqx.at[n, k], qx_s.at[n, k])
+            add(terms.at[order[n] * 4 + column, q_rows, :], rqx.at[n, k])
+
+    weight_terms(0)
+    exchanged(0)
+    sends.send(terms.at[far + x, q_rows, :], rq1.at[0], q1_s.at[0], me.up)
+    sends.send(terms.at[far + me.xp, q_rows, :], rq1.at[1], q1_s.at[1], me.down)
+    weight_terms(1)
+    for n, base, extra, device in ((1, up, x, me.up), (2, down, me.xp, me.down)):
+        exchanged(n)
+        arrive(rq1.at[n - 1], q1_s.at[n - 1])
+        add(terms.at[base + extra, q_rows, :], rq1.at[n - 1])
+        for k, column in enumerate((x, me.xp)):
+            sends.send(terms.at[base + column, q_rows, :], rq2.at[n - 1, k], q2_s.at[n - 1, k], device)
+    weight_terms(2)
+    arrive(rp2.at[0], p2_s.at[0])
+    arrive(rp2.at[1], p2_s.at[1])
+    add(terms.at[pl.ds(own, 4), p_rows, :], rp2.at[0], rp2.at[1])
+    for k, column in enumerate((me.xs, me.xsp)):
+        sends.send(terms.at[own + column, p_rows, :], rpx.at[k], px_s.at[k], me.beside)
+    weight_terms(3)
+    for k, column in enumerate((x, me.xp)):
+        arrive(rqx.at[3, k], qx_s.at[3, k])
+        arrive(rq2.at[0, k], q2_s.at[0, k])
+        arrive(rq2.at[1, k], q2_s.at[1, k])
+        add(terms.at[own + column, q_rows, :], rqx.at[3, k], rq2.at[0, k], rq2.at[1, k])
+        arrive(rpx.at[k], px_s.at[k])
+        add(terms.at[own + column, p_rows, :], rpx.at[k])
+    sends.send(terms.at[own + me.xp], grad_out.at[c], g_s.at[c], me.at(c=t, x=me.xp))
+    src, dst = terms.at[own + x], grad_out.at[c]
+    sends.send(src, dst, g_s.at[c], me.sibling, when=jnp.logical_not(same))
+
+    @pl.when(same)
+    def _():
+        pltpu.make_async_copy(src, dst, g_s.at[c]).start()
+
+    for k in range(8):
+        arrive(rw.at[k], rw_s.at[k])
+    total = rw[0].astype(jnp.float32)
+    for k in range(1, 8):
+        total = total + rw[k].astype(jnp.float32)
+    gq_out[...] = total[:, : 2 * HEAD]
+    gk_out[...] = total[:, 2 * HEAD : 3 * HEAD]
+    gv_out[...] = total[:, 3 * HEAD :]
+    for k in range(16):
+        arrive(attn_out.at[:, pl.ds(k * 2 * HEAD, 2 * HEAD)], attn_s.at[k])
+    for k in range(2):
+        arrive(grad_out.at[k], g_s.at[k])
+    sends.finish()
+
+
+def scatter(attn, dproj, tok, w, piece_rows):
+    f32, bf = jnp.float32, jnp.bfloat16
+    anywhere = pl.BlockSpec(memory_space=pl.ANY)
+    vmem = pl.BlockSpec(memory_space=pltpu.VMEM)
+    dma = pltpu.SemaphoreType.DMA
+    length = attn.shape[0]
+    half = (HALF_ROWS, KH)
+    return pl.pallas_call(
+        scatter_kernel,
+        out_shape=(
+            jax.ShapeDtypeStruct((128, 32 * HEAD), bf),
+            jax.ShapeDtypeStruct((2, 128, KH), bf),
+            jax.ShapeDtypeStruct((piece_rows, 2 * HEAD), f32),
+            jax.ShapeDtypeStruct((piece_rows, HEAD), f32),
+            jax.ShapeDtypeStruct((piece_rows, HEAD), f32),
+        ),
+        in_specs=[anywhere] * 4,
+        out_specs=(anywhere, anywhere, vmem, vmem, vmem),
+        scratch_shapes=[
+            pltpu.VMEM((16, 128, KH), bf),
+            pltpu.VMEM((KH, 8 * HEAD), bf),
+            pltpu.VMEM((length, 8 * HEAD), bf),
+            pltpu.VMEM((16, 128, KH), bf),
+            pltpu.VMEM((4 * piece_rows, 8 * HEAD), bf),
+            pltpu.VMEM((4, 2) + half, bf),
+            pltpu.VMEM((2, 2) + half, bf),
+            pltpu.VMEM((2, 4) + half, bf),
+            pltpu.VMEM((2,) + half, bf),
+            pltpu.VMEM((2,) + half, bf),
+            pltpu.VMEM((2, 2) + half, bf),
+            pltpu.VMEM((8, piece_rows, 4 * HEAD), bf),
+            dma((60,)), dma((16,)), dma((4,)), dma((6,)), dma((4, 2)), dma((2,)), dma((2,)),
+            dma((2,)), dma((2,)), dma((2, 2)), dma((8,)), dma((2,)),
+        ],
+        compiler_params=pltpu.CompilerParams(
+            has_side_effects=True, vmem_limit_bytes=56 * 1024 * 1024
+        ),
+        name="scatter",
+    )(attn, dproj, tok, w)
 
 
 def local(
     tokens, q_weight, key_projection, value_projection, query_norm_gain, key_norm_gain, doc_lengths, out_cot
 ):
-    joined = jnp.concatenate([q_weight, key_projection, value_projection], axis=1)
-    joined = lax.all_gather(joined, "dp", axis=0, tiled=True)
-    row_tokens = lax.all_gather(tokens, "seq", axis=0, tiled=True)
-    cosine, sine, ends = rope_inputs(doc_lengths[0], row_tokens.shape[0])
-    proj = jnp.dot(row_tokens, joined, preferred_element_type=jnp.float32)
-    head_output, dproj = attention(ends, proj, out_cot, cosine, sine, query_norm_gain, key_norm_gain)
-    token_grad = lax.psum_scatter(
-        lax.dot_general(dproj, joined, NT, preferred_element_type=jnp.float32).astype(jnp.bfloat16),
-        "seq",
-        scatter_dimension=0,
-        tiled=True,
+    wj = jnp.concatenate([q_weight, key_projection, value_projection], axis=1)
+    rows, model = tokens.shape
+    half = model // 2
+    tok2 = jnp.pad(
+        tokens.reshape(rows, 2, half).transpose(1, 0, 2), ((0, 0), (0, 0), (0, KH - half))
     )
-    weight_terms = lax.dot_general(
-        row_tokens, dproj, (((0,), (0,)), ((), ())), preferred_element_type=jnp.float32
-    ).astype(jnp.bfloat16)
-    grads = lax.psum_scatter(weight_terms, "dp", scatter_dimension=0, tiled=True).astype(jnp.float32)
-    attn_out = lax.all_to_all(head_output, "seq", split_axis=0, concat_axis=1, tiled=True)
-    qc = q_weight.shape[1]
-    kc = key_projection.shape[1]
-    return (attn_out, token_grad, grads[:, :qc], grads[:, qc : qc + kc], grads[:, qc + kc :])
+    same = (lax.axis_index("dp") % 2 == (lax.axis_index("seq") % 4) // 2).astype(jnp.int32)
+    docs = jnp.concatenate([doc_lengths[0], same[None], jnp.zeros((123,), jnp.int32)])
+    docs = jnp.broadcast_to(docs[None, :], (8, 128))
+    cosine, sine = rope_inputs(out_cot.shape[0])
+    proj, tok, w, cot2, docs2 = gather(tok2, wj, out_cot, docs)
+    attn, dproj = attention(
+        docs, docs2, proj, out_cot, cot2, cosine, sine, query_norm_gain, key_norm_gain
+    )
+    attn_out, grad, gq, gk, gv = scatter(attn, dproj, tok, w, wj.shape[0])
+    token_grad = jnp.concatenate([grad[0, :, :half], grad[1, :, :half]], axis=1)
+    return (attn_out, token_grad, gq, gk, gv)
 
 
 def solution(mesh):

time: 323 us -> 209 us (0.65)
  the two profiles are of different devices: /device:TPU:33 before, /device:TPU:45 now
where the time goes in v2:
time: 209 us
  Pallas kernels  190 us (91%)
  local copies, waits for them, and re-layouts  10.5 us (5%)
  other arithmetic  7.85 us (4%)
    pallas_call x1, Pallas kernels, scatter(): pl.pallas_call(scatter_kernel, out_shape=(jax.ShapeDtypeStruct((128, 32 *...  98 us
    pallas_call x1, Pallas kernels, gather(): pl.pallas_call(gather_kernel, out_shape=(jax.ShapeDtypeStruct((length, 4...  58.1 us
    pallas_call x1, Pallas kernels, attention(): pl.pallas_call(attention_kernel, out_shape=(jax.ShapeDtypeStruct((length,...  33.5 us
    unnamed x27, local copies, waits for them, and re-layouts  7.38 us

profile of v2, /device:TPU:45, one launch (start us, length us, event | category | flops | bytes accessed | tf_op | source)
XLA Modules:
  0.0 208.8 jit_solution(14950391966277990096)
XLA Ops:
  0.7 0.7 pad_add_fusion
  1.4 0.6 broadcast_in_dim.20.docs.docs_ref
  2.0 1.8 pad_maximum_fusion.3.wj
  3.8 1.4 copy.13
  5.2 0.4 copy.14
  5.6 0.9 pad.4.tok2
  6.5 3.7 %fusion = (f32[2048,64]{1,0:T(8,128)S(1)}, f32[2048,64]{1,0:T(8,128)S(1)}, f32[2048,64]{1,0:T(8,128)S(1)}) fusion(f32[64]{0:T(128)S(1)} %multiply_power_fusion, f32[2048]{0:T(1024)S(1)} %iota_convert_fusion), kind=kLoop, calls=%fused_computation.8 | loop fusion | flops 262144 | bytes 1581312 | tf_op jit(solution)/shard_map/neg | solution.py:34
  10.2 0.6 pad_maximum_fusion
  10.9 0.0 copy-start
  10.9 0.0 copy-start.3
  10.9 0.0 copy-start.5
  10.9 0.0 copy-start.6
  10.9 58.1 %gather.1 = (f32[2048,512]{1,0:T(8,128)}, bf16[16,128,1408]{2,1,0:T(8,128)(2,1)}, bf16[1408,1024]{1,0:T(8,128)(2,1)}, bf16[2048,256]{1,0:T(8,128)(2,1)}, s32[8,128]{1,0:T(8,128)}) custom-call(bf16[2,128,1408]{2,1,0:T(8,128)(2,1)} %pad.4.tok2, bf16[336,512]{1,0:T(8,128)(2,1)} %pad_maximum_fusion.3.wj, bf16[2048,256]{1,0:T(8,128)(2,1)} %cot_own.1, ...), custom_call_target="tpu_custom_call" | custom-call | tf_op jit(solution)/shard_map/gather/pallas_call | solution.py:397
  69.0 0.0 copy-done
  69.0 0.0 copy-done.3
  69.0 0.0 copy-done.5
  69.1 0.0 copy-done.6
  69.1 0.0 copy-start.2
  69.1 1.2 copy-done.2
  70.3 0.7 copy-done.4
  71.0 33.5 %attention.1 = (bf16[2048,256]{1,0:T(8,128)(2,1)S(1)}, bf16[2048,512]{1,0:T(8,128)(2,1)}) custom-call(s32[8,128]{1,0:T(8,128)S(1)} %copy-done.3, s32[8,128]{1,0:T(8,128)S(1)} %copy-done.4, f32[2048,512]{1,0:T(8,128)} %get-tuple-element.18.proj_ref, bf16[2048,256]{1,0:T(8,128)(2,1)S(1)} %copy-done, bf16[2048,256]{1,0:T(8,128)(2,1)S(1)} %copy-done.2, ...), custom_call_target="tpu_custom_call" | custom-call | tf_op jit(solution)/shard_map/attention/pallas_call | solution.py:171
  104.5 0.0 copy-start.1
  104.5 1.0 copy-done.1
  105.4 98.0 %scatter.1 = (bf16[128,4096]{1,0:T(8,128)(2,1)}, bf16[2,128,1408]{2,1,0:T(8,128)(2,1)}, f32[336,256]{1,0:T(8,128)}, f32[336,128]{1,0:T(8,128)}, f32[336,128]{1,0:T(8,128)}) custom-call(bf16[2048,256]{1,0:T(8,128)(2,1)} %copy-done.1, bf16[2048,512]{1,0:T(8,128)(2,1)} %get-tuple-element.21.dproj, bf16[16,128,1408]{2,1,0:T(8,128)(2,1)} %get-tuple-element.22.tok_in, ...), custom_call_target="tpu_custom_call" | custom-call | tf_op jit(solution)/shard_map/scatter/pallas_call | solution.py:575
  203.5 0.0 copy-start.7
  203.5 1.2 slice_bitcast_fusion.1
  204.8 1.0 pad_maximum_fusion.2
  205.8 0.0 copy-done.7
  205.8 1.0 copy.19
  206.7 0.7 copy.20
  207.5 0.7 copy.21
  208.1 0.7 copy.22
  (10 shorter events, 0.0 us)
Async XLA Ops:
  10.9 58.2 %copy-start = (bf16[2048,256]{1,0:T(8,128)(2,1)S(1)}, bf16[2048,256]{1,0:T(8,128)(2,1)}, u32[]{:S(2)}) copy-start(bf16[2048,256]{1,0:T(8,128)(2,1)} %cot_own.1) | copy-start | bytes 3145732
  10.9 58.2 %copy-start.3 = (s32[8,128]{1,0:T(8,128)S(1)}, s32[8,128]{1,0:T(8,128)}, u32[]{:S(2)}) copy-start(s32[8,128]{1,0:T(8,128)} %broadcast_in_dim.20.docs.docs_ref) | copy-start | bytes 12292
  10.9 58.2 %copy-start.5 = (f32[128]{0:T(128)S(1)}, f32[128]{0:T(128)}, u32[]{:S(2)}) copy-start(f32[128]{0:T(128)} %param.12) | copy-start | bytes 1540
  10.9 58.2 %copy-start.6 = (f32[128]{0:T(128)S(1)}, f32[128]{0:T(128)}, u32[]{:S(2)}) copy-start(f32[128]{0:T(128)} %param.13) | copy-start | bytes 1540
  69.1 1.2 copy-start.2
  70.3 0.7 copy-start.4
  104.5 1.0 copy-start.1
  203.5 2.3 %copy-start.7 = (bf16[128,4096]{1,0:T(8,128)(2,1)S(1)}, bf16[128,4096]{1,0:T(8,128)(2,1)}, u32[]{:S(2)}) copy-start(bf16[128,4096]{1,0:T(8,128)(2,1)} %get-tuple-element.41) | copy-start | bytes 3145732
  204.7 2.0 copy-start.8
  204.7 2.7 %copy-start.10 = (f32[336,128]{1,0:T(8,128)S(1)}, f32[336,128]{1,0:T(8,128)}, u32[]{:S(2)}) copy-start(f32[336,128]{1,0:T(8,128)} %get-tuple-element.44) | copy-start | bytes 516100
  204.7 3.4 %copy-start.9 = (f32[336,128]{1,0:T(8,128)S(1)}, f32[336,128]{1,0:T(8,128)}, u32[]{:S(2)}) copy-start(f32[336,128]{1,0:T(8,128)} %get-tuple-element.45) | copy-start | bytes 516100

commit v3 on v2

--- a/solution.py
+++ b/solution.py
@@ -3,6 +3,7 @@
 
 import jax
 import jax.numpy as jnp
+import numpy as np
 from jax import lax
 from jax.experimental import pallas as pl
 from jax.experimental.pallas import tpu as pltpu
@@ -23,16 +24,15 @@
     return lax.dot_general(a, b, dims, preferred_element_type=jnp.float32)
 
 
-def rope_inputs(length):
-    position = jnp.arange(length, dtype=jnp.int32)
-    half = HEAD // 2
-    inverse = rope_base ** (-jnp.arange(half, dtype=jnp.float32) * (2.0 / HEAD))
-    angle = position.astype(jnp.float32)[:, None] * inverse[None, :]
-    cosine, sine = jnp.cos(angle), jnp.sin(angle)
-    return (
-        jnp.concatenate([cosine, cosine], axis=1),
-        jnp.concatenate([-sine, sine], axis=1),
-    )
+def rope_tables(blocks):
+    inverse = rope_base ** (-np.arange(HEAD // 2) * (2.0 / HEAD))
+    inverse = np.concatenate([inverse, inverse])[None, :]
+    coarse = (np.arange(blocks) * BLOCK)[:, None] * inverse
+    fine = np.arange(BLOCK)[:, None] * inverse
+    return [
+        jnp.asarray(table, jnp.float32)
+        for table in (np.cos(coarse), np.sin(coarse), np.cos(fine), np.sin(fine))
+    ]
 
 
 def norm_factor(x):
@@ -55,13 +55,20 @@
 
 
 def attention_kernel(
-    docs_ref, docs2_ref, proj_ref, cot_own, cot_got, cos_ref, sin_ref, gq_ref, gk_ref, out_ref, dproj_ref,
+    docs_ref, docs2_ref, proj_ref, cot_own, cot_got, cos_a, sin_a, cos_b, sin_b, gq_ref, gk_ref, out_ref, dproj_ref,
     cot_ref, cot_sem, q_s, k_s, kt_s, v_s, vt_s, e_s, eb_s, dk_s, dv_s, acc_s, dot_s, row_s,
 ):
     length = proj_ref.shape[0]
     blocks = length // BLOCK
     span = WINDOW // BLOCK
-    same = docs_ref[0, 4] == 1
+    same = lax.axis_index("dp") % 2 == (lax.axis_index("seq") % 4) // 2
+    lane = lax.broadcasted_iota(jnp.int32, (1, HEAD), 1)
+    sign = jnp.where(lane < HEAD // 2, -1.0, 1.0)
+
+    def tables(i):
+        ca, sa = cos_a[pl.ds(i, 1), :], sin_a[pl.ds(i, 1), :]
+        return ca * cos_b[...] - sa * sin_b[...], (sa * sign) * cos_b[...] + (ca * sign) * sin_b[...]
+
     pl.when(same)(lambda: pltpu.make_async_copy(cot_own, cot_ref, cot_sem).start())
     pl.when(jnp.logical_not(same))(lambda: pltpu.make_async_copy(cot_got, cot_ref, cot_sem).start())
     e0, e1, e2 = [jnp.where(same, docs_ref[0, k], docs2_ref[0, k]) for k in range(3)]
@@ -78,7 +85,7 @@
     @pl.loop(0, blocks)
     def _(i):
         rows = pl.ds(pl.multiple_of(i * BLOCK, BLOCK), BLOCK)
-        cosine, sine = cos_ref[rows, :], sin_ref[rows, :]
+        cosine, sine = tables(i)
         for h in range(2):
             x = proj_ref[rows, h * HEAD : (h + 1) * HEAD]
             n = x * norm_factor(x) * gq_ref[...]
@@ -111,17 +118,26 @@
         row_s[...] = jnp.zeros_like(row_s)
         query = q_s[i]
 
-        @pl.loop(first, i + 1)
-        def _(j):
+        last = q0 + BLOCK - 1
+        whole = jnp.maximum(start_of(last), last - (WINDOW - 1))
+
+        def forward(j, masked):
             slot = j - i + span
-            s = mm(k_s[j], query, NT)
-            key_pos = j * BLOCK + lax.broadcasted_iota(jnp.int32, (BLOCK, 2 * BLOCK), 0)
-            e = jnp.where((key_pos >= low2) & (key_pos <= token2), jnp.exp2(s * exp_scale), 0.0)
+            e = jnp.exp2(mm(k_s[j], query, NT) * exp_scale)
+            if masked:
+                key_pos = j * BLOCK + lax.broadcasted_iota(jnp.int32, (BLOCK, 2 * BLOCK), 0)
+                e = jnp.where((key_pos >= low2) & (key_pos <= token2), e, 0.0)
             e_s[slot] = e
             eb = e.astype(jnp.bfloat16)
             eb_s[slot] = eb
             row_s[...] += jnp.sum(e.reshape(BLOCK // 8, 8, 2 * BLOCK), axis=0)
             acc_s[...] += mm(vt_s[j], eb)
+
+        @pl.loop(first, i + 1)
+        def _(j):
+            free = (j * BLOCK >= whole) & (j < i)
+            pl.when(free)(lambda: forward(j, False))
+            pl.when(jnp.logical_not(free))(lambda: forward(j, True))
 
         inv = 1.0 / jnp.sum(row_s[...], axis=0, keepdims=True)
         out_t = acc_s[...] * inv
@@ -145,7 +161,7 @@
             dk_s[j] += mm(ds, query)
             acc_s[...] += mm(kt_s[j], ds)
 
-        cosine, sine = cos_ref[rows, :], sin_ref[rows, :]
+        cosine, sine = tables(i)
         for h in range(2):
             g = acc_s[:, h * BLOCK : (h + 1) * BLOCK].T * score_scale
             x = proj_ref[rows, h * HEAD : (h + 1) * HEAD]
@@ -155,14 +171,14 @@
     @pl.loop(0, blocks)
     def _(i):
         rows = pl.ds(pl.multiple_of(i * BLOCK, BLOCK), BLOCK)
-        cosine, sine = cos_ref[rows, :], sin_ref[rows, :]
+        cosine, sine = tables(i)
         x = proj_ref[rows, 2 * HEAD : 3 * HEAD]
         dx = norm_back(rotate_back(dk_s[i] * score_scale, cosine, sine), x, gk_ref[...])
         dproj_ref[rows, 2 * HEAD : 3 * HEAD] = dx.astype(jnp.bfloat16)
         dproj_ref[rows, 3 * HEAD : 4 * HEAD] = dv_s[i].astype(jnp.bfloat16)
 
 
-def attention(docs, docs2, proj, cot, cot2, cosine, sine, gain_q, gain_k):
+def attention(docs, docs2, proj, cot, cot2, gain_q, gain_k):
     length = proj.shape[0]
     blocks = length // BLOCK
     slots = WINDOW // BLOCK + 1
@@ -176,7 +192,7 @@
         ),
         in_specs=[pl.BlockSpec(memory_space=pltpu.SMEM)] * 2
         + [vmem, pl.BlockSpec(memory_space=pl.ANY), pl.BlockSpec(memory_space=pl.ANY)]
-        + [vmem] * 4,
+        + [vmem] * 6,
         out_specs=(vmem, vmem),
         scratch_shapes=[
             pltpu.VMEM((length, 2 * HEAD), bf),
@@ -194,13 +210,14 @@
             pltpu.VMEM((HEAD, 2 * BLOCK), bf),
             pltpu.VMEM((8, 2 * BLOCK), f32),
         ],
-        compiler_params=pltpu.CompilerParams(vmem_limit_bytes=48 * 1024 * 1024),
+        compiler_params=pltpu.CompilerParams(vmem_limit_bytes=60 * 1024 * 1024),
         name="attention",
-    )(docs, docs2, proj, cot, cot2, cosine, sine, gain_q.reshape(1, HEAD), gain_k.reshape(1, HEAD))
+    )(docs, docs2, proj, cot, cot2, *rope_tables(blocks), gain_q.reshape(1, HEAD), gain_k.reshape(1, HEAD))
 
 
 MESH = pl.DeviceIdType.MESH
 KH = 1408
+PAD = 64
 HALF_ROWS = 64
 
 
@@ -259,8 +276,8 @@
 
 
 def gather_kernel(
-    tok2, wj, cot, docs, proj_out, tok_out, w_out, cot_out, docs_out,
-    tok, w, wx, other, sib, send_s, p_s, q_s, first_s, w_s, misc_s, sib_s, local_s,
+    tokens, wq, wk, wv, cot, docs, proj_out, tok_out, w_out, cot_out, docs_out,
+    tok, w, wj, wx, other, sib, send_s, p_s, q_s, first_s, w_s, misc_s, sib_s, local_s, join_s,
 ):
     me = Place()
     z, c, y, x, t, same = me.z, me.c, me.y, me.x, me.t, me.same
@@ -268,6 +285,12 @@
     width = 4 * HEAD
     part = {"p": (pl.ds(0, HALF_ROWS), p_s), "q": (pl.ds(HALF_ROWS, HALF_ROWS), q_s)}
     piece_rows = wj.shape[0]
+    joins = [
+        pltpu.make_async_copy(src, wj.at[:, pl.ds(low, src.shape[1])], join_s.at[k])
+        for k, (src, low) in enumerate(((wq, 0), (wk, 2 * HEAD), (wv, 3 * HEAD)))
+    ]
+    for join in joins:
+        join.start()
 
     def forward(name, slot, device):
         rows, sems = part[name]
@@ -283,11 +306,15 @@
     first = first_s.at[jnp.where(same, 0, 1)]
     for k in range(2):
         local = same & (c == k)
-        sends.send(tok2.at[k], tok.at[own], first, me.at(c=k, x=target_x), when=jnp.logical_not(local))
+        src = tokens.at[:, pl.ds(k * (tokens.shape[1] - KH), KH)]
+        sends.send(src, tok.at[own], first, me.at(c=k, x=target_x), when=jnp.logical_not(local))
 
         @pl.when(local)
         def _():
-            pltpu.make_async_copy(tok2.at[k], tok.at[own], first_s.at[0]).start()
+            pltpu.make_async_copy(src, tok.at[own], first_s.at[0]).start()
+
+    for join in joins:
+        join.wait()
 
     sends.send(wj, wx, misc_s.at[0], me.at(x=me.xp))
     sends.send(docs, docs_out, misc_s.at[2], me.sibling)
@@ -296,7 +323,7 @@
     piece = (z % 2) * 2 + c
 
     def spread(src, g):
-        rows = pl.ds(pl.multiple_of(piece * piece_rows, 16), piece_rows)
+        rows = pl.ds(pl.multiple_of(target_c * PAD + piece * piece_rows, 16), piece_rows)
         dst = w.at[rows, pl.ds(pl.multiple_of(g * width, width), width)]
         sem = w_s.at[piece * 2 + g]
         here = target_c == c
@@ -308,7 +335,9 @@
         def _():
             pltpu.make_async_copy(src, dst, sem).start()
 
-    w[pl.ds(4 * piece_rows, KH - 4 * piece_rows), :] = jnp.zeros((KH - 4 * piece_rows, 2 * width), jnp.bfloat16)
+    w[pl.ds(pl.multiple_of((1 - c) * 4 * piece_rows, PAD), PAD), :] = jnp.zeros((PAD, 2 * width), jnp.bfloat16)
+    below, above, far = me.down_y * 4, me.up_y * 4, me.far_y * 4
+    here, beside = (x, me.xp), (me.xs, me.xsp)
     for slot, sem in ((own, 0), (pair, 1)):
         arrive(tok.at[slot], first_s.at[sem])
         forward("q", slot, me.up)
@@ -319,68 +348,70 @@
         forward("q", slot, me.beside)
         if sem == 0:
             spread(wj, t)
+            landed("q", below + x)
+            forward("q", below + x, me.up)
+            forward("q", below + x, me.beside)
     arrive(wx, misc_s.at[0])
     spread(wx, 1 - t)
     swap = jnp.logical_not(same)
     sends.send(cot, cot_out, misc_s.at[1], me.at(c=1 - c, x=me.xp), when=swap)
-
-    for column in (me.xs, me.xsp):
-        slot = y * 4 + column
-        landed("p", slot)
-        forward("p", slot, me.up)
-        forward("p", slot, me.down)
-    below, above, far = me.down_y * 4, me.up_y * 4, me.far_y * 4
-    landed("q", below + x)
-    forward("q", below + x, me.up)
-    forward("q", below + x, me.beside)
+    landed("q", above + x)
+    forward("q", above + x, me.beside)
     landed("q", above + me.xp)
     forward("q", above + me.xp, me.down)
     forward("q", above + me.xp, me.beside)
     landed("q", below + me.xp)
     forward("q", below + me.xp, me.beside)
-    landed("q", above + x)
-    forward("q", above + x, me.beside)
-    for column in (x, me.xp):
+    for column in beside:
+        landed("p", y * 4 + column)
+        forward("p", y * 4 + column, me.up)
+        forward("p", y * 4 + column, me.down)
+    for column in here:
         landed("p", below + column)
         forward("p", below + column, me.up)
-    for column in (me.xs, me.xsp):
+        landed("q", far + column)
+        forward("q", far + column, me.beside)
+    for column in beside:
         landed("p", above + column)
         forward("p", above + column, me.down)
-    for column in (x, me.xp):
-        landed("q", far + column)
-        forward("q", far + column, me.beside)
 
     for i in range(4):
         for g in range(2):
-            arrive(
-                w.at[pl.ds(i * piece_rows, piece_rows), pl.ds(g * width, width)], w_s.at[i * 2 + g]
-            )
+            arrive(w.at[pl.ds(i * piece_rows, piece_rows), pl.ds(g * width, width)], w_s.at[i * 2 + g])
     pltpu.make_async_copy(w, w_out, local_s.at[4]).start()
 
-    beside = (me.xs, me.xsp)
-    here = (x, me.xp)
     plan = (
-        (me.y, (), beside),
-        (me.down_y, beside, beside),
-        (me.up_y, here, beside),
-        (me.far_y, here + beside, beside),
+        (0, "p", ()),
+        (0, "q", beside),
+        (1, "q", beside),
+        (2, "q", beside),
+        (1, "p", beside),
+        (2, "p", here),
+        (3, "p", here + beside),
+        (3, "q", beside),
     )
-    for n, (row, need_p, need_q) in enumerate(plan):
-        for column in need_p:
-            landed("p", row * 4 + column)
-        for column in need_q:
-            landed("q", row * 4 + column)
+    lines = (y, me.down_y, me.up_y, me.far_y)
+    done = [0, 0, 0, 0]
+    units = []
+    for n, (line, name, need) in enumerate(plan):
+        row = lines[line]
+        for column in need:
+            landed(name, row * 4 + column)
         slots = pl.ds(pl.multiple_of(row * 4, 4), 4)
-        rows = pl.ds(pl.multiple_of(row * 512, 512), 512)
-        pltpu.make_async_copy(tok.at[slots], tok_out.at[slots], local_s.at[n]).start()
-        block = tok[slots].reshape(512, KH)
-        other[rows, :] = mm(block, w[:, pl.ds(pl.multiple_of((1 - c) * width, width), width)])
-        sends.send(other.at[rows, :], sib.at[rows, :], sib_s.at[n], me.sibling)
-        proj_out[rows, :] = mm(block, w[:, pl.ds(pl.multiple_of(c * width, width), width)])
-    for n, (row, _, _) in enumerate(plan):
-        rows = pl.ds(pl.multiple_of(row * 512, 512), 512)
-        arrive(sib.at[rows, :], sib_s.at[n])
-        proj_out[rows, :] += sib[rows, :]
+        done[line] += 1
+        if done[line] == 2:
+            pltpu.make_async_copy(tok.at[slots], tok_out.at[slots], local_s.at[line]).start()
+        rows = part[name][0]
+        block = tok[slots, rows, :].reshape(4 * HALF_ROWS, KH)
+        shape = (4, HALF_ROWS, width)
+        other[slots, rows, :] = mm(block, w[:, pl.ds(pl.multiple_of((1 - c) * width, width), width)]).reshape(shape)
+        sends.send(other.at[slots, rows, :], sib.at[slots, rows, :], sib_s.at[n], me.sibling)
+        proj_out[slots, rows, :] = mm(block, w[:, pl.ds(pl.multiple_of(c * width, width), width)]).reshape(shape)
+        units.append((slots, rows))
+    for n, (slots, rows) in enumerate(units):
+        arrive(sib.at[slots, rows, :], sib_s.at[n])
+        proj_out[slots, rows, :] += sib[slots, rows, :]
+    for n, row in enumerate(lines):
         slots = pl.ds(pl.multiple_of(row * 4, 4), 4)
         pltpu.make_async_copy(tok.at[slots], tok_out.at[slots], local_s.at[n]).wait()
     pltpu.make_async_copy(w, w_out, local_s.at[4]).wait()
@@ -389,41 +420,41 @@
     sends.finish()
 
 
-def gather(tok2, wj, cot, docs):
+def gather(tokens, wq, wk, wv, cot, docs):
     f32, bf = jnp.float32, jnp.bfloat16
     anywhere = pl.BlockSpec(memory_space=pl.ANY)
     dma = pltpu.SemaphoreType.DMA
-    length = cot.shape[0]
     return pl.pallas_call(
         gather_kernel,
         out_shape=(
-            jax.ShapeDtypeStruct((length, 4 * HEAD), f32),
+            jax.ShapeDtypeStruct((16, 128, 4 * HEAD), f32),
             jax.ShapeDtypeStruct((16, 128, KH), bf),
             jax.ShapeDtypeStruct((KH, 8 * HEAD), bf),
             jax.ShapeDtypeStruct(cot.shape, bf),
             jax.ShapeDtypeStruct(docs.shape, docs.dtype),
         ),
-        in_specs=[anywhere] * 4,
+        in_specs=[anywhere] * 6,
         out_specs=(pl.BlockSpec(memory_space=pltpu.VMEM),) + (anywhere,) * 4,
         scratch_shapes=[
             pltpu.VMEM((16, 128, KH), bf),
             pltpu.VMEM((KH, 8 * HEAD), bf),
-            pltpu.VMEM(wj.shape, bf),
-            pltpu.VMEM((length, 4 * HEAD), f32),
-            pltpu.VMEM((length, 4 * HEAD), f32),
-            dma((60,)), dma((16,)), dma((16,)), dma((2,)), dma((8,)), dma((3,)), dma((4,)), dma((5,)),
+            pltpu.VMEM((wq.shape[0], 4 * HEAD), bf),
+            pltpu.VMEM((wq.shape[0], 4 * HEAD), bf),
+            pltpu.VMEM((16, 128, 4 * HEAD), f32),
+            pltpu.VMEM((16, 128, 4 * HEAD), f32),
+            dma((64,)), dma((16,)), dma((16,)), dma((2,)), dma((8,)), dma((3,)), dma((8,)), dma((5,)), dma((3,)),
         ],
         compiler_params=pltpu.CompilerParams(
-            has_side_effects=True, vmem_limit_bytes=56 * 1024 * 1024
+            has_side_effects=True, vmem_limit_bytes=60 * 1024 * 1024
         ),
         name="gather",
-    )(tok2, wj, cot, docs)
+    )(tokens, wq, wk, wv, cot, docs)
 
 
 def scatter_kernel(
     attn, dproj, tok_in, w_in, attn_out, grad_out, gq_out, gk_out, gv_out,
-    tok, w, dpj, terms, dw, rqx, rp1, rp2, rpx, rq1, rq2, rw,
-    send_s, attn_s, dp_s, local_s, qx_s, p1_s, p2_s, px_s, q1_s, q2_s, rw_s, g_s,
+    tok, w, dpj, terms, dw, rqx, rp1, rp2, rpx, rq1, rq2, rw, rwx, wsum,
+    send_s, attn_s, dp_s, local_s, qx_s, p1_s, p2_s, px_s, q1_s, q2_s, rw_s, g_s, rwx_s,
 ):
     me = Place()
     z, c, y, x, t, same = me.z, me.c, me.y, me.x, me.t, me.same
@@ -460,20 +491,40 @@
         for k, column in enumerate((me.xs, me.xsp)):
             sends.send(terms.at[row * 4 + column, q_rows, :], rqx.at[n, k], qx_s.at[n, k], me.beside)
 
+    def weight_terms(i):
+        if i == 0:
+            arrive(tok, local_s.at[5])
+        low, high = ((0, 512), (512, 768), (768, 1152), (1152, KH))[i]
+        left = tok[:, :, low:high].reshape(16 * 128, high - low)
+        dw[low:high, :] = mm(left, dpj[...], (((0,), (0,)), ((), ()))).astype(jnp.bfloat16)
+        for g in range(2):
+            rows = pl.ds(pl.multiple_of(c * PAD + i * piece_rows, 16), piece_rows)
+            src = dw.at[rows, pl.ds(g * width, width)]
+            dst, sem = rw.at[z * 2 + g], rw_s.at[z * 2 + g]
+            to_z, to_c = 2 * c + i // 2, i % 2
+            stays = (to_z == z) & (c == to_c)
+            sends.send(src, dst, sem, me.at(z=to_z, c=to_c), when=jnp.logical_not(stays))
+
+            @pl.when(stays)
+            def _():
+                pltpu.make_async_copy(src, dst, sem).start()
+
+    def exchanged(n):
+        for k, column in enumerate((x, me.xp)):
+            arrive(rqx.at[n, k], qx_s.at[n, k])
+            add(terms.at[order[n] * 4 + column, q_rows, :], rqx.at[n, k])
+
+    def finish(n, rows):
+        src, dst, sem = terms.at[own + me.xp, rows, :], grad_out.at[c, rows, :], g_s.at[c, n]
+        sends.send(src, dst, sem, me.at(c=t, x=me.xp))
+        src = terms.at[own + x, rows, :]
+        sends.send(src, dst, sem, me.sibling, when=jnp.logical_not(same))
+
+        @pl.when(same)
+        def _():
+            pltpu.make_async_copy(src, dst, sem).start()
+
     far, up, down, own = me.far_y * 4, me.up_y * 4, me.down_y * 4, y * 4
-    compute(0)
-    sends.send(terms.at[pl.ds(far, 2), p_rows, :], rp1.at[0], p1_s.at[0], me.up)
-    sends.send(terms.at[pl.ds(far + 2, 2), p_rows, :], rp1.at[1], p1_s.at[1], me.down)
-    compute(1)
-    compute(2)
-    compute(3)
-    arrive(rp1.at[0], p1_s.at[0])
-    add(terms.at[pl.ds(up, 2), p_rows, :], rp1.at[0])
-    sends.send(terms.at[pl.ds(up, 4), p_rows, :], rp2.at[0], p2_s.at[0], me.up)
-    arrive(rp1.at[1], p1_s.at[1])
-    add(terms.at[pl.ds(down + 2, 2), p_rows, :], rp1.at[1])
-    sends.send(terms.at[pl.ds(down, 4), p_rows, :], rp2.at[1], p2_s.at[1], me.down)
-
     group = y * 4 + jnp.where(same, x, me.xp)
     columns = pl.ds(pl.multiple_of(group * 2 * HEAD, 2 * HEAD), 2 * HEAD)
     for dy in range(4):
@@ -490,78 +541,68 @@
             else:
                 sends.send(src, dst, attn_s.at[group], me.at(c=t, y=to_y, x=to_x))
 
-    def weight_terms(i):
-        if i == 0:
-            arrive(tok, local_s.at[5])
-        low, high = i * 384, min(KH, i * 384 + 384)
-        cut = min(high, 4 * piece_rows)
-        left = tok[:, :, low:high].reshape(16 * 128, high - low)
-        term = mm(left, dpj[...], (((0,), (0,)), ((), ())))
-        dw[low:cut, :] = term[: cut - low].astype(jnp.bfloat16)
-        for g in range(2):
-            src = dw.at[pl.ds(i * piece_rows, piece_rows), pl.ds(g * width, width)]
-            dst, sem = rw.at[z * 2 + t], rw_s.at[z * 2 + t]
-            to_z, to_c = 2 * c + i // 2, i % 2
-            stays = (to_z == z) & (c == to_c) & (t == g)
-            sends.send(
-                src, dst, sem, me.at(z=to_z, c=to_c, x=jnp.where(t == g, x, me.xp)),
-                when=jnp.logical_not(stays),
-            )
-
-            @pl.when(stays)
-            def _():
-                pltpu.make_async_copy(src, dst, sem).start()
-
-    def exchanged(n):
-        for k, column in enumerate((x, me.xp)):
-            arrive(rqx.at[n, k], qx_s.at[n, k])
-            add(terms.at[order[n] * 4 + column, q_rows, :], rqx.at[n, k])
-
+    compute(0)
+    sends.send(terms.at[pl.ds(far, 2), p_rows, :], rp1.at[0], p1_s.at[0], me.up)
+    sends.send(terms.at[pl.ds(far + 2, 2), p_rows, :], rp1.at[1], p1_s.at[1], me.down)
+    compute(1)
+    compute(2)
+    compute(3)
     weight_terms(0)
+    weight_terms(1)
+    arrive(rp1.at[0], p1_s.at[0])
+    add(terms.at[pl.ds(up, 2), p_rows, :], rp1.at[0])
+    sends.send(terms.at[pl.ds(up, 4), p_rows, :], rp2.at[0], p2_s.at[0], me.up)
+    arrive(rp1.at[1], p1_s.at[1])
+    add(terms.at[pl.ds(down + 2, 2), p_rows, :], rp1.at[1])
+    sends.send(terms.at[pl.ds(down, 4), p_rows, :], rp2.at[1], p2_s.at[1], me.down)
+    weight_terms(2)
+    weight_terms(3)
     exchanged(0)
     sends.send(terms.at[far + x, q_rows, :], rq1.at[0], q1_s.at[0], me.up)
     sends.send(terms.at[far + me.xp, q_rows, :], rq1.at[1], q1_s.at[1], me.down)
-    weight_terms(1)
     for n, base, extra, device in ((1, up, x, me.up), (2, down, me.xp, me.down)):
         exchanged(n)
         arrive(rq1.at[n - 1], q1_s.at[n - 1])
         add(terms.at[base + extra, q_rows, :], rq1.at[n - 1])
         for k, column in enumerate((x, me.xp)):
             sends.send(terms.at[base + column, q_rows, :], rq2.at[n - 1, k], q2_s.at[n - 1, k], device)
-    weight_terms(2)
     arrive(rp2.at[0], p2_s.at[0])
     arrive(rp2.at[1], p2_s.at[1])
     add(terms.at[pl.ds(own, 4), p_rows, :], rp2.at[0], rp2.at[1])
     for k, column in enumerate((me.xs, me.xsp)):
         sends.send(terms.at[own + column, p_rows, :], rpx.at[k], px_s.at[k], me.beside)
-    weight_terms(3)
+
+    def summed(g):
+        total = rw[g].astype(jnp.float32)
+        for k in range(1, 4):
+            total = total + rw[2 * k + g].astype(jnp.float32)
+        return total
+
+    for k in range(8):
+        arrive(rw.at[k], rw_s.at[k])
+    wsum[...] = summed(1 - t).astype(jnp.bfloat16)
+    sends.send(wsum, rwx, rwx_s.at[0], me.at(x=me.xp))
     for k, column in enumerate((x, me.xp)):
         arrive(rqx.at[3, k], qx_s.at[3, k])
         arrive(rq2.at[0, k], q2_s.at[0, k])
         arrive(rq2.at[1, k], q2_s.at[1, k])
         add(terms.at[own + column, q_rows, :], rqx.at[3, k], rq2.at[0, k], rq2.at[1, k])
+    finish(1, q_rows)
+    for k, column in enumerate((x, me.xp)):
         arrive(rpx.at[k], px_s.at[k])
         add(terms.at[own + column, p_rows, :], rpx.at[k])
-    sends.send(terms.at[own + me.xp], grad_out.at[c], g_s.at[c], me.at(c=t, x=me.xp))
-    src, dst = terms.at[own + x], grad_out.at[c]
-    sends.send(src, dst, g_s.at[c], me.sibling, when=jnp.logical_not(same))
-
-    @pl.when(same)
-    def _():
-        pltpu.make_async_copy(src, dst, g_s.at[c]).start()
-
-    for k in range(8):
-        arrive(rw.at[k], rw_s.at[k])
-    total = rw[0].astype(jnp.float32)
-    for k in range(1, 8):
-        total = total + rw[k].astype(jnp.float32)
+    finish(0, p_rows)
+    total = summed(t)
+    arrive(rwx, rwx_s.at[0])
+    total = total + rwx[...].astype(jnp.float32)
     gq_out[...] = total[:, : 2 * HEAD]
     gk_out[...] = total[:, 2 * HEAD : 3 * HEAD]
     gv_out[...] = total[:, 3 * HEAD :]
     for k in range(16):
         arrive(attn_out.at[:, pl.ds(k * 2 * HEAD, 2 * HEAD)], attn_s.at[k])
     for k in range(2):
-        arrive(grad_out.at[k], g_s.at[k])
+        for n, rows in ((0, p_rows), (1, q_rows)):
+            arrive(grad_out.at[k, rows, :], g_s.at[k, n])
     sends.finish()
 
 
@@ -588,7 +629,7 @@
             pltpu.VMEM((KH, 8 * HEAD), bf),
             pltpu.VMEM((length, 8 * HEAD), bf),
             pltpu.VMEM((16, 128, KH), bf),
-            pltpu.VMEM((4 * piece_rows, 8 * HEAD), bf),
+            pltpu.VMEM((KH, 8 * HEAD), bf),
             pltpu.VMEM((4, 2) + half, bf),
             pltpu.VMEM((2, 2) + half, bf),
             pltpu.VMEM((2, 4) + half, bf),
@@ -596,11 +637,13 @@
             pltpu.VMEM((2,) + half, bf),
             pltpu.VMEM((2, 2) + half, bf),
             pltpu.VMEM((8, piece_rows, 4 * HEAD), bf),
+            pltpu.VMEM((piece_rows, 4 * HEAD), bf),
+            pltpu.VMEM((piece_rows, 4 * HEAD), bf),
             dma((60,)), dma((16,)), dma((4,)), dma((6,)), dma((4, 2)), dma((2,)), dma((2,)),
-            dma((2,)), dma((2,)), dma((2, 2)), dma((8,)), dma((2,)),
+            dma((2,)), dma((2,)), dma((2, 2)), dma((8,)), dma((2, 2)), dma((1,)),
         ],
         compiler_params=pltpu.CompilerParams(
-            has_side_effects=True, vmem_limit_bytes=56 * 1024 * 1024
+            has_side_effects=True, vmem_limit_bytes=60 * 1024 * 1024
         ),
         name="scatter",
     )(attn, dproj, tok, w)
@@ -609,22 +652,16 @@
 def local(
     tokens, q_weight, key_projection, value_projection, query_norm_gain, key_norm_gain, doc_lengths, out_cot
 ):
-    wj = jnp.concatenate([q_weight, key_projection, value_projection], axis=1)
-    rows, model = tokens.shape
-    half = model // 2
-    tok2 = jnp.pad(
-        tokens.reshape(rows, 2, half).transpose(1, 0, 2), ((0, 0), (0, 0), (0, KH - half))
+    half = tokens.shape[1] // 2
+    proj, tok, w, cot2, docs2 = gather(
+        tokens, q_weight, key_projection, value_projection, out_cot, doc_lengths
     )
-    same = (lax.axis_index("dp") % 2 == (lax.axis_index("seq") % 4) // 2).astype(jnp.int32)
-    docs = jnp.concatenate([doc_lengths[0], same[None], jnp.zeros((123,), jnp.int32)])
-    docs = jnp.broadcast_to(docs[None, :], (8, 128))
-    cosine, sine = rope_inputs(out_cot.shape[0])
-    proj, tok, w, cot2, docs2 = gather(tok2, wj, out_cot, docs)
+    proj = proj.reshape(out_cot.shape[0], 4 * HEAD)
     attn, dproj = attention(
-        docs, docs2, proj, out_cot, cot2, cosine, sine, query_norm_gain, key_norm_gain
+        doc_lengths, docs2, proj, out_cot, cot2, query_norm_gain, key_norm_gain
     )
-    attn_out, grad, gq, gk, gv = scatter(attn, dproj, tok, w, wj.shape[0])
-    token_grad = jnp.concatenate([grad[0, :, :half], grad[1, :, :half]], axis=1)
+    attn_out, grad, gq, gk, gv = scatter(attn, dproj, tok, w, q_weight.shape[0])
+    token_grad = jnp.concatenate([grad[0, :, :half], grad[1, :, PAD:]], axis=1)
     return (attn_out, token_grad, gq, gk, gv)
 
 

time: 209 us -> 181 us (0.87)
  the two profiles are of different devices: /device:TPU:45 before, /device:TPU:33 now
where the time goes in v3:
time: 181 us
  Pallas kernels  174 us (96%)
  local copies, waits for them, and re-layouts  4.4 us (2%)
    pallas_call x1, Pallas kernels, scatter(): pl.pallas_call(scatter_kernel, out_shape=(jax.ShapeDtypeStruct((128, 32 *...  79.6 us
    pallas_call x1, Pallas kernels, gather(): pl.pallas_call(gather_kernel, out_shape=(jax.ShapeDtypeStruct((16, 128, 4...  58 us
    pallas_call x1, Pallas kernels, attention(): pl.pallas_call(attention_kernel, out_shape=(jax.ShapeDtypeStruct((length,...  36.8 us

profile of v3, /device:TPU:33, one launch (start us, length us, event | category | flops | bytes accessed | tf_op | source)
XLA Modules:
  0.0 180.6 jit_solution(10193940170192877493)
XLA Ops:
  0.6 58.0 %gather.1 = (f32[16,128,512]{2,1,0:T(8,128)}, bf16[16,128,1408]{2,1,0:T(8,128)(2,1)}, bf16[1408,1024]{1,0:T(8,128)(2,1)}, bf16[2048,256]{1,0:T(8,128)(2,1)}, s32[1,4]{1,0:T(1,128)}) custom-call(bf16[128,2688]{1,0:T(8,128)(2,1)} %tokens.1, bf16[336,256]{1,0:T(8,128)(2,1)} %wq.1, bf16[336,128]{1,0:T(8,128)(2,1)} %wk.1, bf16[336,128]{1,0:T(8,128)(2,1)} %wv.1, ...), custom_call_target="tpu_custom_call" | custom-call | tf_op jit(solution)/shard_map/gather/pallas_call | solution.py:427
  58.7 36.8 %attention.1 = (bf16[2048,256]{1,0:T(8,128)(2,1)}, bf16[2048,512]{1,0:T(8,128)(2,1)}) custom-call(s32[1,4]{1,0:T(1,128)} %docs_ref.1, s32[1,4]{1,0:T(1,128)} %get-tuple-element.17.docs2_ref, f32[2048,512]{1,0:T(8,128)} %bitcast.7, bf16[2048,256]{1,0:T(8,128)(2,1)} %cot_own.1, bf16[2048,256]{1,0:T(8,128)(2,1)} %get-tuple-element.19.cot_got, ...), custom_call_target="tpu_custom_call" | custom-call | tf_op jit(solution)/shard_map/attention/pallas_call | solution.py:187
  95.5 79.6 %scatter.1 = (bf16[128,4096]{1,0:T(8,128)(2,1)}, bf16[2,128,1408]{2,1,0:T(8,128)(2,1)}, f32[336,256]{1,0:T(8,128)}, f32[336,128]{1,0:T(8,128)}, f32[336,128]{1,0:T(8,128)}) custom-call(bf16[2048,256]{1,0:T(8,128)(2,1)} %get-tuple-element.20.attn, bf16[2048,512]{1,0:T(8,128)(2,1)} %get-tuple-element.21.dproj, ...), custom_call_target="tpu_custom_call" | custom-call | tf_op jit(solution)/shard_map/scatter/pallas_call | solution.py:616
  175.1 0.0 copy-start
  175.2 1.3 slice_bitcast_fusion.1
  176.5 0.0 copy-start.1
  176.5 0.0 copy-start.3
  176.5 0.0 copy-start.2
  176.5 1.0 pad_maximum_fusion
  177.5 0.0 copy-done
  177.5 1.0 copy.21
  178.5 0.0 copy-done.1
  178.5 0.7 copy.22
  179.3 0.0 copy-done.3
  179.3 0.7 copy.23
  179.9 0.0 copy-done.2
  179.9 0.7 copy.24
Async XLA Ops:
  175.1 2.4 %copy-start = (bf16[128,4096]{1,0:T(8,128)(2,1)S(1)}, bf16[128,4096]{1,0:T(8,128)(2,1)}, u32[]{:S(2)}) copy-start(bf16[128,4096]{1,0:T(8,128)(2,1)} %get-tuple-element.36) | copy-start | bytes 3145732
  176.5 2.0 %copy-start.1 = (f32[336,256]{1,0:T(8,128)S(1)}, f32[336,256]{1,0:T(8,128)}, u32[]{:S(2)}) copy-start(f32[336,256]{1,0:T(8,128)} %get-tuple-element.38) | copy-start | bytes 1032196
  176.5 2.7 %copy-start.3 = (f32[336,128]{1,0:T(8,128)S(1)}, f32[336,128]{1,0:T(8,128)}, u32[]{:S(2)}) copy-start(f32[336,128]{1,0:T(8,128)} %get-tuple-element.39) | copy-start | bytes 516100
  176.5 3.4 %copy-start.2 = (f32[336,128]{1,0:T(8,128)S(1)}, f32[336,128]{1,0:T(8,128)}, u32[]{:S(2)}) copy-start(f32[336,128]{1,0:T(8,128)} %get-tuple-element.40) | copy-start | bytes 516100

commit v4 on v3

--- a/solution.py
+++ b/solution.py
@@ -94,10 +94,10 @@
         n = x * norm_factor(x) * gk_ref[...]
         key = rotate(n, cosine, sine)
         k_s[i] = key.astype(jnp.bfloat16)
-        kt_s[i] = key.T.astype(jnp.bfloat16)
+        kt_s[i] = key.astype(jnp.bfloat16).T
         value = proj_ref[rows, 3 * HEAD : 4 * HEAD]
         v_s[i] = value.astype(jnp.bfloat16)
-        vt_s[i] = value.T.astype(jnp.bfloat16)
+        vt_s[i] = value.astype(jnp.bfloat16).T
         dk_s[i] = jnp.zeros((BLOCK, HEAD), jnp.float32)
         dv_s[i] = jnp.zeros((BLOCK, HEAD), jnp.float32)
 
@@ -142,14 +142,15 @@
         inv = 1.0 / jnp.sum(row_s[...], axis=0, keepdims=True)
         out_t = acc_s[...] * inv
         dot = jnp.concatenate(
-            [cot_ref[rows, h * HEAD : (h + 1) * HEAD].astype(jnp.float32).T for h in range(2)], axis=1
+            [cot_ref[rows, h * HEAD : (h + 1) * HEAD].T.astype(jnp.float32) for h in range(2)], axis=1
         )
         for h in range(2):
             out_ref[rows, h * HEAD : (h + 1) * HEAD] = (
-                out_t[:, h * BLOCK : (h + 1) * BLOCK].T.astype(jnp.bfloat16)
+                out_t[:, h * BLOCK : (h + 1) * BLOCK].astype(jnp.bfloat16).T
             )
         delta = jnp.sum(out_t * dot, axis=0, keepdims=True) * inv
         dot_s[...] = (dot * inv).astype(jnp.bfloat16)
+        dout = dot_s[...].T
         acc_s[...] = jnp.zeros_like(acc_s)
 
         @pl.loop(first, i + 1)
@@ -157,7 +158,7 @@
             slot = j - i + span
             dp = mm(v_s[j], dot_s[...])
             ds = (e_s[slot] * (dp - delta)).astype(jnp.bfloat16)
-            dv_s[j] += mm(eb_s[slot], dot_s[...], NT)
+            dv_s[j] += mm(eb_s[slot], dout)
             dk_s[j] += mm(ds, query)
             acc_s[...] += mm(kt_s[j], ds)
 
@@ -244,6 +245,13 @@
         return (z * 2 + c, y * 4 + x)
 
 
+def meet(devices):
+    barrier = pltpu.get_barrier_semaphore()
+    for device in devices:
+        pl.semaphore_signal(barrier, inc=1, device_id=device, device_id_type=MESH)
+    pl.semaphore_wait(barrier, len(devices))
+
+
 class Sends:
     def __init__(self, sems):
         self.sems, self.count, self.open = sems, 0, []
@@ -291,6 +299,10 @@
     ]
     for join in joins:
         join.start()
+    meet(
+        [me.sibling, me.beside, me.up, me.down, me.at(c=0, x=me.xp), me.at(c=1, x=me.xp)]
+        + [me.at(z=(z + k) % 4, c=core) for k in (1, 2, 3) for core in range(2)]
+    )
 
     def forward(name, slot, device):
         rows, sems = part[name]
@@ -445,7 +457,7 @@
             dma((64,)), dma((16,)), dma((16,)), dma((2,)), dma((8,)), dma((3,)), dma((8,)), dma((5,)), dma((3,)),
         ],
         compiler_params=pltpu.CompilerParams(
-            has_side_effects=True, vmem_limit_bytes=60 * 1024 * 1024
+            collective_id=0, has_side_effects=True, vmem_limit_bytes=60 * 1024 * 1024
         ),
         name="gather",
     )(tokens, wq, wk, wv, cot, docs)
@@ -466,6 +478,14 @@
     piece_rows = gq_out.shape[0]
 
     pltpu.make_async_copy(w_in, w, local_s.at[4]).start()
+    meet(
+        [me.sibling]
+        + [
+            me.at(c=core, y=(y + dy) % 4, x=(x + dx) % 4)
+            for dy in range(4) for dx in range(4) if dy or dx for core in range(2)
+        ]
+        + [me.at(z=(z + k) % 4, c=core) for k in (1, 2, 3) for core in range(2)]
+    )
     for n, row in enumerate(order):
         rows = pl.ds(pl.multiple_of(row * 512, 512), 512)
         pltpu.make_async_copy(dproj.at[rows, :], dpj.at[rows, mine], local_s.at[n]).start()
@@ -643,7 +663,7 @@
             dma((2,)), dma((2,)), dma((2, 2)), dma((8,)), dma((2, 2)), dma((1,)),
         ],
         compiler_params=pltpu.CompilerParams(
-            has_side_effects=True, vmem_limit_bytes=60 * 1024 * 1024
+            collective_id=1, has_side_effects=True, vmem_limit_bytes=60 * 1024 * 1024
         ),
         name="scatter",
     )(attn, dproj, tok, w)

time: 181 us -> 168 us (0.928)
  Pallas kernels: 174 us -> 163 us
    pallas_call x1, Pallas kernels: 58 us -> 51.8 us  [gather(): pl.pallas_call(gather_kernel, out_shape=(jax.ShapeDtypeStruct((16, 128, 4...]
    pallas_call x1, Pallas kernels: 36.8 us -> 33.3 us  [attention(): pl.pallas_call(attention_kernel, out_shape=(jax.ShapeDtypeStruct((length,...]
    pallas_call x1, Pallas kernels: 79.6 us -> 77.6 us  [scatter(): pl.pallas_call(scatter_kernel, out_shape=(jax.ShapeDtypeStruct((128, 32 *...]
where the time goes in v4:
time: 168 us; the launch traced here: 169 us
  Pallas kernels  163 us (97%)
  local copies, waits for them, and re-layouts  4.4 us (3%)
    pallas_call x1, Pallas kernels, scatter(): pl.pallas_call(scatter_kernel, out_shape=(jax.ShapeDtypeStruct((128, 32 *...  77.6 us
    pallas_call x1, Pallas kernels, gather(): pl.pallas_call(gather_kernel, out_shape=(jax.ShapeDtypeStruct((16, 128, 4...  51.8 us
    pallas_call x1, Pallas kernels, attention(): pl.pallas_call(attention_kernel, out_shape=(jax.ShapeDtypeStruct((length,...  33.3 us

profile of v4, /device:TPU:33, one launch (start us, length us, event | category | flops | bytes accessed | tf_op | source)
XLA Modules:
  0.0 168.9 jit_solution(9437993655371585122)
XLA Ops:
  0.6 51.8 %gather.1 = (f32[16,128,512]{2,1,0:T(8,128)}, bf16[16,128,1408]{2,1,0:T(8,128)(2,1)}, bf16[1408,1024]{1,0:T(8,128)(2,1)}, bf16[2048,256]{1,0:T(8,128)(2,1)}, s32[1,4]{1,0:T(1,128)}) custom-call(bf16[128,2688]{1,0:T(8,128)(2,1)} %tokens.1, bf16[336,256]{1,0:T(8,128)(2,1)} %wq.1, bf16[336,128]{1,0:T(8,128)(2,1)} %wk.1, bf16[336,128]{1,0:T(8,128)(2,1)} %wv.1, ...), custom_call_target="tpu_custom_call" | custom-call | tf_op jit(solution)/shard_map/gather/pallas_call | solution.py:439
  52.4 33.3 %attention.1 = (bf16[2048,256]{1,0:T(8,128)(2,1)}, bf16[2048,512]{1,0:T(8,128)(2,1)}) custom-call(s32[1,4]{1,0:T(1,128)} %docs_ref.1, s32[1,4]{1,0:T(1,128)} %get-tuple-element.17.docs2_ref, f32[2048,512]{1,0:T(8,128)} %bitcast.7, bf16[2048,256]{1,0:T(8,128)(2,1)} %cot_own.1, bf16[2048,256]{1,0:T(8,128)(2,1)} %get-tuple-element.19.cot_got, ...), custom_call_target="tpu_custom_call" | custom-call | tf_op jit(solution)/shard_map/attention/pallas_call | solution.py:188
  85.8 77.6 %scatter.1 = (bf16[128,4096]{1,0:T(8,128)(2,1)}, bf16[2,128,1408]{2,1,0:T(8,128)(2,1)}, f32[336,256]{1,0:T(8,128)}, f32[336,128]{1,0:T(8,128)}, f32[336,128]{1,0:T(8,128)}) custom-call(bf16[2048,256]{1,0:T(8,128)(2,1)} %get-tuple-element.20.attn, bf16[2048,512]{1,0:T(8,128)(2,1)} %get-tuple-element.21.dproj, ...), custom_call_target="tpu_custom_call" | custom-call | tf_op jit(solution)/shard_map/scatter/pallas_call | solution.py:636
  163.4 0.0 copy-start
  163.4 1.3 slice_bitcast_fusion.1
  164.8 0.0 copy-start.1
  164.8 0.0 copy-start.3
  164.8 0.0 copy-start.2
  164.8 1.0 pad_maximum_fusion
  165.8 0.0 copy-done
  165.8 1.0 copy.21
  166.8 0.0 copy-done.1
  166.8 0.7 copy.22
  167.5 0.0 copy-done.3
  167.5 0.7 copy.23
  168.2 0.0 copy-done.2
  168.2 0.7 copy.24
Async XLA Ops:
  163.4 2.4 %copy-start = (bf16[128,4096]{1,0:T(8,128)(2,1)S(1)}, bf16[128,4096]{1,0:T(8,128)(2,1)}, u32[]{:S(2)}) copy-start(bf16[128,4096]{1,0:T(8,128)(2,1)} %get-tuple-element.36) | copy-start | bytes 3145732
  164.8 2.0 %copy-start.1 = (f32[336,256]{1,0:T(8,128)S(1)}, f32[336,256]{1,0:T(8,128)}, u32[]{:S(2)}) copy-start(f32[336,256]{1,0:T(8,128)} %get-tuple-element.38) | copy-start | bytes 1032196
  164.8 2.7 %copy-start.3 = (f32[336,128]{1,0:T(8,128)S(1)}, f32[336,128]{1,0:T(8,128)}, u32[]{:S(2)}) copy-start(f32[336,128]{1,0:T(8,128)} %get-tuple-element.39) | copy-start | bytes 516100
  164.8 3.4 %copy-start.2 = (f32[336,128]{1,0:T(8,128)S(1)}, f32[336,128]{1,0:T(8,128)}, u32[]{:S(2)}) copy-start(f32[336,128]{1,0:T(8,128)} %get-tuple-element.40) | copy-start | bytes 516100

commit v5 on v4

--- a/solution.py
+++ b/solution.py
@@ -12,6 +12,7 @@
 HEAD = 128
 WINDOW = 1024
 BLOCK = 256
+UNROLL = 2
 score_scale = 168.0 ** (-0.5)
 exp_scale = score_scale * math.log2(math.e)
 rope_base = 10000.0
@@ -55,12 +56,30 @@
 
 
 def attention_kernel(
-    docs_ref, docs2_ref, proj_ref, cot_own, cot_got, cos_a, sin_a, cos_b, sin_b, gq_ref, gk_ref, out_ref, dproj_ref,
-    cot_ref, cot_sem, q_s, k_s, kt_s, v_s, vt_s, e_s, eb_s, dk_s, dv_s, acc_s, dot_s, row_s,
+    docs_ref, docs2_ref, proj_hbm, cot_own, cot_got, cos_a, sin_a, cos_b, sin_b, gq_ref, gk_ref, out_hbm, dproj_hbm,
+    cot_ref, cot_sem, proj_ref, out_ref, dproj_ref, in_sem, out_sem, q_s, k_s, kt_s, v_s, vt_s, e_s, eb_s, dk_s, dv_s, acc_s, dot_s, row_s,
 ):
-    length = proj_ref.shape[0]
+    length = proj_hbm.shape[0]
     blocks = length // BLOCK
     span = WINDOW // BLOCK
+    def block_rows(i):
+        return pl.ds(pl.multiple_of(i * BLOCK, BLOCK), BLOCK)
+
+    def load(i):
+        rows = block_rows(i)
+        return pltpu.make_async_copy(proj_hbm.at[rows, :], proj_ref.at[rows, :], in_sem.at[i])
+
+    def store(i, k):
+        rows = block_rows(i)
+        src, dst, cols = (
+            (out_ref, out_hbm, pl.ds(0, 2 * HEAD)),
+            (dproj_ref, dproj_hbm, pl.ds(0, 2 * HEAD)),
+            (dproj_ref, dproj_hbm, pl.ds(2 * HEAD, 2 * HEAD)),
+        )[k]
+        return pltpu.make_async_copy(src.at[rows, cols], dst.at[rows, cols], out_sem.at[i, k])
+
+    for i in range(blocks):
+        load(i).start()
     same = lax.axis_index("dp") % 2 == (lax.axis_index("seq") % 4) // 2
     lane = lax.broadcasted_iota(jnp.int32, (1, HEAD), 1)
     sign = jnp.where(lane < HEAD // 2, -1.0, 1.0)
@@ -84,6 +103,7 @@
 
     @pl.loop(0, blocks)
     def _(i):
+        load(i).wait()
         rows = pl.ds(pl.multiple_of(i * BLOCK, BLOCK), BLOCK)
         cosine, sine = tables(i)
         for h in range(2):
@@ -118,26 +138,26 @@
         row_s[...] = jnp.zeros_like(row_s)
         query = q_s[i]
 
-        last = q0 + BLOCK - 1
-        whole = jnp.maximum(start_of(last), last - (WINDOW - 1))
-
-        def forward(j, masked):
-            slot = j - i + span
-            e = jnp.exp2(mm(k_s[j], query, NT) * exp_scale)
-            if masked:
-                key_pos = j * BLOCK + lax.broadcasted_iota(jnp.int32, (BLOCK, 2 * BLOCK), 0)
+        steps = (i - first + UNROLL) // UNROLL
+        start = i + 1 - steps * UNROLL
+
+        @pl.loop(0, steps)
+        def _(step):
+            low_j = start + step * UNROLL
+            keys = [jnp.maximum(low_j + u, 0) for u in range(UNROLL)]
+            total, mixed = row_s[...], acc_s[...]
+            scores = [mm(k_s[j], query, NT) for j in keys]
+            for u, j in enumerate(keys):
+                slot = low_j + u - i + span + UNROLL - 1
+                key_pos = (low_j + u) * BLOCK + lax.broadcasted_iota(jnp.int32, (BLOCK, 2 * BLOCK), 0)
+                e = jnp.exp2(scores[u] * exp_scale)
                 e = jnp.where((key_pos >= low2) & (key_pos <= token2), e, 0.0)
-            e_s[slot] = e
-            eb = e.astype(jnp.bfloat16)
-            eb_s[slot] = eb
-            row_s[...] += jnp.sum(e.reshape(BLOCK // 8, 8, 2 * BLOCK), axis=0)
-            acc_s[...] += mm(vt_s[j], eb)
-
-        @pl.loop(first, i + 1)
-        def _(j):
-            free = (j * BLOCK >= whole) & (j < i)
-            pl.when(free)(lambda: forward(j, False))
-            pl.when(jnp.logical_not(free))(lambda: forward(j, True))
+                e_s[slot] = e
+                eb = e.astype(jnp.bfloat16)
+                eb_s[slot] = eb
+                total += jnp.sum(e.reshape(BLOCK // 8, 8, 2 * BLOCK), axis=0)
+                mixed += mm(vt_s[j], eb)
+            row_s[...], acc_s[...] = total, mixed
 
         inv = 1.0 / jnp.sum(row_s[...], axis=0, keepdims=True)
         out_t = acc_s[...] * inv
@@ -148,19 +168,28 @@
             out_ref[rows, h * HEAD : (h + 1) * HEAD] = (
                 out_t[:, h * BLOCK : (h + 1) * BLOCK].astype(jnp.bfloat16).T
             )
+        store(i, 0).start()
         delta = jnp.sum(out_t * dot, axis=0, keepdims=True) * inv
         dot_s[...] = (dot * inv).astype(jnp.bfloat16)
         dout = dot_s[...].T
         acc_s[...] = jnp.zeros_like(acc_s)
 
-        @pl.loop(first, i + 1)
-        def _(j):
-            slot = j - i + span
-            dp = mm(v_s[j], dot_s[...])
-            ds = (e_s[slot] * (dp - delta)).astype(jnp.bfloat16)
-            dv_s[j] += mm(eb_s[slot], dout)
-            dk_s[j] += mm(ds, query)
-            acc_s[...] += mm(kt_s[j], ds)
+        @pl.loop(0, steps)
+        def _(step):
+            low_j = start + step * UNROLL
+            keys = [jnp.maximum(low_j + u, 0) for u in range(UNROLL)]
+            slots = [low_j + u - i + span + UNROLL - 1 for u in range(UNROLL)]
+            d_probs = [mm(v_s[j], dot_s[...]) for j in keys]
+            d_scores = [(e_s[slot] * (dp - delta)).astype(jnp.bfloat16) for slot, dp in zip(slots, d_probs)]
+            d_values = [mm(eb_s[slot], dout) for slot in slots]
+            d_keys = [mm(ds, query) for ds in d_scores]
+            mixed = acc_s[...]
+            for j, ds in zip(keys, d_scores):
+                mixed += mm(kt_s[j], ds)
+            acc_s[...] = mixed
+            for j, dv, dk in zip(keys, d_values, d_keys):
+                dv_s[j] += dv
+                dk_s[j] += dk
 
         cosine, sine = tables(i)
         for h in range(2):
@@ -168,6 +197,7 @@
             x = proj_ref[rows, h * HEAD : (h + 1) * HEAD]
             dx = norm_back(rotate_back(g, cosine, sine), x, gq_ref[...])
             dproj_ref[rows, h * HEAD : (h + 1) * HEAD] = dx.astype(jnp.bfloat16)
+        store(i, 1).start()
 
     @pl.loop(0, blocks)
     def _(i):
@@ -177,12 +207,17 @@
         dx = norm_back(rotate_back(dk_s[i] * score_scale, cosine, sine), x, gk_ref[...])
         dproj_ref[rows, 2 * HEAD : 3 * HEAD] = dx.astype(jnp.bfloat16)
         dproj_ref[rows, 3 * HEAD : 4 * HEAD] = dv_s[i].astype(jnp.bfloat16)
+        store(i, 2).start()
+
+    for i in range(blocks):
+        for k in range(3):
+            store(i, k).wait()
 
 
 def attention(docs, docs2, proj, cot, cot2, gain_q, gain_k):
     length = proj.shape[0]
     blocks = length // BLOCK
-    slots = WINDOW // BLOCK + 1
+    slots = WINDOW // BLOCK + UNROLL
     vmem = pl.BlockSpec(memory_space=pltpu.VMEM)
     bf, f32 = jnp.bfloat16, jnp.float32
     return pl.pallas_call(
@@ -192,12 +227,17 @@
             jax.ShapeDtypeStruct((length, 4 * HEAD), bf),
         ),
         in_specs=[pl.BlockSpec(memory_space=pltpu.SMEM)] * 2
-        + [vmem, pl.BlockSpec(memory_space=pl.ANY), pl.BlockSpec(memory_space=pl.ANY)]
+        + [pl.BlockSpec(memory_space=pl.ANY)] * 3
         + [vmem] * 6,
-        out_specs=(vmem, vmem),
+        out_specs=(pl.BlockSpec(memory_space=pl.ANY), pl.BlockSpec(memory_space=pl.ANY)),
         scratch_shapes=[
             pltpu.VMEM((length, 2 * HEAD), bf),
             pltpu.SemaphoreType.DMA(()),
+            pltpu.VMEM((length, 4 * HEAD), f32),
+            pltpu.VMEM((length, 2 * HEAD), bf),
+            pltpu.VMEM((length, 4 * HEAD), bf),
+            pltpu.SemaphoreType.DMA((blocks,)),
+            pltpu.SemaphoreType.DMA((blocks, 3)),
             pltpu.VMEM((blocks, 2 * BLOCK, HEAD), bf),
             pltpu.VMEM((blocks, BLOCK, HEAD), bf),
             pltpu.VMEM((blocks, HEAD, BLOCK), bf),
@@ -284,8 +324,8 @@
 
 
 def gather_kernel(
-    tokens, wq, wk, wv, cot, docs, proj_out, tok_out, w_out, cot_out, docs_out,
-    tok, w, wj, wx, other, sib, send_s, p_s, q_s, first_s, w_s, misc_s, sib_s, local_s, join_s,
+    tokens, wq, wk, wv, cot, docs, proj_hbm, tok_out, w_out, cot_out, docs_out,
+    tok, w, wj, wx, other, sib, send_s, p_s, q_s, first_s, w_s, misc_s, sib_s, local_s, join_s, proj_out, proj_s,
 ):
     me = Place()
     z, c, y, x, t, same = me.z, me.c, me.y, me.x, me.t, me.same
@@ -405,6 +445,15 @@
     lines = (y, me.down_y, me.up_y, me.far_y)
     done = [0, 0, 0, 0]
     units = []
+
+    def complete(n):
+        slots, rows = units[n]
+        arrive(sib.at[slots, rows, :], sib_s.at[n])
+        proj_out[slots, rows, :] += sib[slots, rows, :]
+        pltpu.make_async_copy(
+            proj_out.at[slots, rows, :], proj_hbm.at[slots, rows, :], proj_s.at[n]
+        ).start()
+
     for n, (line, name, need) in enumerate(plan):
         row = lines[line]
         for column in need:
@@ -420,9 +469,13 @@
         sends.send(other.at[slots, rows, :], sib.at[slots, rows, :], sib_s.at[n], me.sibling)
         proj_out[slots, rows, :] = mm(block, w[:, pl.ds(pl.multiple_of(c * width, width), width)]).reshape(shape)
         units.append((slots, rows))
+        if n:
+            complete(n - 1)
+    complete(len(plan) - 1)
     for n, (slots, rows) in enumerate(units):
-        arrive(sib.at[slots, rows, :], sib_s.at[n])
-        proj_out[slots, rows, :] += sib[slots, rows, :]
+        pltpu.make_async_copy(
+            proj_out.at[slots, rows, :], proj_hbm.at[slots, rows, :], proj_s.at[n]
+        ).wait()
     for n, row in enumerate(lines):
         slots = pl.ds(pl.multiple_of(row * 4, 4), 4)
         pltpu.make_async_copy(tok.at[slots], tok_out.at[slots], local_s.at[n]).wait()
@@ -446,7 +499,7 @@
             jax.ShapeDtypeStruct(docs.shape, docs.dtype),
         ),
         in_specs=[anywhere] * 6,
-        out_specs=(pl.BlockSpec(memory_space=pltpu.VMEM),) + (anywhere,) * 4,
+        out_specs=(anywhere,) * 5,
         scratch_shapes=[
             pltpu.VMEM((16, 128, KH), bf),
             pltpu.VMEM((KH, 8 * HEAD), bf),
@@ -455,6 +508,7 @@
             pltpu.VMEM((16, 128, 4 * HEAD), f32),
             pltpu.VMEM((16, 128, 4 * HEAD), f32),
             dma((64,)), dma((16,)), dma((16,)), dma((2,)), dma((8,)), dma((3,)), dma((8,)), dma((5,)), dma((3,)),
+            pltpu.VMEM((16, 128, 4 * HEAD), f32), dma((8,)),
         ],
         compiler_params=pltpu.CompilerParams(
             collective_id=0, has_side_effects=True, vmem_limit_bytes=60 * 1024 * 1024
@@ -464,8 +518,8 @@
 
 
 def scatter_kernel(
-    attn, dproj, tok_in, w_in, attn_out, grad_out, gq_out, gk_out, gv_out,
-    tok, w, dpj, terms, dw, rqx, rp1, rp2, rpx, rq1, rq2, rw, rwx, wsum,
+    attn, dproj, tok_in, w_in, attn_out, token_out, gq_out, gk_out, gv_out,
+    tok, w, dpj, terms, dw, rqx, rp1, rp2, rpx, rq1, rq2, rw, rwx, wsum, grad_out,
     send_s, attn_s, dp_s, local_s, qx_s, p1_s, p2_s, px_s, q1_s, q2_s, rw_s, g_s, rwx_s,
 ):
     me = Place()
@@ -547,20 +601,6 @@
     far, up, down, own = me.far_y * 4, me.up_y * 4, me.down_y * 4, y * 4
     group = y * 4 + jnp.where(same, x, me.xp)
     columns = pl.ds(pl.multiple_of(group * 2 * HEAD, 2 * HEAD), 2 * HEAD)
-    for dy in range(4):
-        for dx in range(4):
-            to_y, to_x = (y + dy) % 4, (x + dx) % 4
-            rows = pl.ds(pl.multiple_of((to_y * 4 + to_x) * 128, 128), 128)
-            src, dst = attn.at[rows, :], attn_out.at[:, columns]
-            if dy == 0 and dx == 0:
-                sends.send(src, dst, attn_s.at[group], me.sibling, when=jnp.logical_not(same))
-
-                @pl.when(same)
-                def _():
-                    pltpu.make_async_copy(src, dst, attn_s.at[group]).start()
-            else:
-                sends.send(src, dst, attn_s.at[group], me.at(c=t, y=to_y, x=to_x))
-
     compute(0)
     sends.send(terms.at[pl.ds(far, 2), p_rows, :], rp1.at[0], p1_s.at[0], me.up)
     sends.send(terms.at[pl.ds(far + 2, 2), p_rows, :], rp1.at[1], p1_s.at[1], me.down)
@@ -598,6 +638,20 @@
             total = total + rw[2 * k + g].astype(jnp.float32)
         return total
 
+    for dy in range(4):
+        for dx in range(4):
+            to_y, to_x = (y + dy) % 4, (x + dx) % 4
+            rows = pl.ds(pl.multiple_of((to_y * 4 + to_x) * 128, 128), 128)
+            src, dst = attn.at[rows, :], attn_out.at[:, columns]
+            if dy == 0 and dx == 0:
+                sends.send(src, dst, attn_s.at[group], me.sibling, when=jnp.logical_not(same))
+
+                @pl.when(same)
+                def _():
+                    pltpu.make_async_copy(src, dst, attn_s.at[group]).start()
+            else:
+                sends.send(src, dst, attn_s.at[group], me.at(c=t, y=to_y, x=to_x))
+
     for k in range(8):
         arrive(rw.at[k], rw_s.at[k])
     wsum[...] = summed(1 - t).astype(jnp.bfloat16)
@@ -623,6 +677,11 @@
     for k in range(2):
         for n, rows in ((0, p_rows), (1, q_rows)):
             arrive(grad_out.at[k, rows, :], g_s.at[k, n])
+    low = token_out.shape[1] - KH
+    lane = lax.broadcasted_iota(jnp.int32, (128, KH - low), 1)
+    token_out[:, :low] = grad_out[0, :, :low]
+    token_out[:, low:KH] = jnp.where(lane < PAD, grad_out[0, :, low:], grad_out[1, :, : KH - low])
+    token_out[:, KH:] = grad_out[1, :, KH - low :]
     sends.finish()
 
 
@@ -637,13 +696,13 @@
         scatter_kernel,
         out_shape=(
             jax.ShapeDtypeStruct((128, 32 * HEAD), bf),
-            jax.ShapeDtypeStruct((2, 128, KH), bf),
+            jax.ShapeDtypeStruct((128, 2 * (KH - PAD)), bf),
             jax.ShapeDtypeStruct((piece_rows, 2 * HEAD), f32),
             jax.ShapeDtypeStruct((piece_rows, HEAD), f32),
             jax.ShapeDtypeStruct((piece_rows, HEAD), f32),
         ),
         in_specs=[anywhere] * 4,
-        out_specs=(anywhere, anywhere, vmem, vmem, vmem),
+        out_specs=(anywhere, vmem, vmem, vmem, vmem),
         scratch_shapes=[
             pltpu.VMEM((16, 128, KH), bf),
             pltpu.VMEM((KH, 8 * HEAD), bf),
@@ -659,6 +718,7 @@
             pltpu.VMEM((8, piece_rows, 4 * HEAD), bf),
             pltpu.VMEM((piece_rows, 4 * HEAD), bf),
             pltpu.VMEM((piece_rows, 4 * HEAD), bf),
+            pltpu.VMEM((2, 128, KH), bf),
             dma((60,)), dma((16,)), dma((4,)), dma((6,)), dma((4, 2)), dma((2,)), dma((2,)),
             dma((2,)), dma((2,)), dma((2, 2)), dma((8,)), dma((2, 2)), dma((1,)),
         ],
@@ -672,7 +732,6 @@
 def local(
     tokens, q_weight, key_projection, value_projection, query_norm_gain, key_norm_gain, doc_lengths, out_cot
 ):
-    half = tokens.shape[1] // 2
     proj, tok, w, cot2, docs2 = gather(
         tokens, q_weight, key_projection, value_projection, out_cot, doc_lengths
     )
@@ -680,8 +739,7 @@
     attn, dproj = attention(
         doc_lengths, docs2, proj, out_cot, cot2, query_norm_gain, key_norm_gain
     )
-    attn_out, grad, gq, gk, gv = scatter(attn, dproj, tok, w, q_weight.shape[0])
-    token_grad = jnp.concatenate([grad[0, :, :half], grad[1, :, PAD:]], axis=1)
+    attn_out, token_grad, gq, gk, gv = scatter(attn, dproj, tok, w, q_weight.shape[0])
     return (attn_out, token_grad, gq, gk, gv)
 
 

time: 168 us -> 165 us (0.982); the launches traced: 169 us -> 164 us
  Pallas kernels: 163 us -> 156 us
  local copies, waits for them, and re-layouts: 4.4 us -> 7.4 us
    pallas_call x1, Pallas kernels: 77.6 us -> 71.3 us  [scatter(): pl.pallas_call(scatter_kernel, out_shape=(jax.ShapeDtypeStruct((128, 32 *...]
    unnamed x12 -> x9, local copies, waits for them, and re-layouts: 3.05 us -> 7.4 us
where the time goes in v5:
time: 165 us; the launch traced here: 164 us
  Pallas kernels  156 us (95%)
  local copies, waits for them, and re-layouts  7.4 us (4%)
    pallas_call x1, Pallas kernels, scatter(): pl.pallas_call(scatter_kernel, out_shape=(jax.ShapeDtypeStruct((128, 32 *...  71.3 us
    pallas_call x1, Pallas kernels, gather(): pl.pallas_call(gather_kernel, out_shape=(jax.ShapeDtypeStruct((16, 128, 4...  51.3 us
    pallas_call x1, Pallas kernels, attention(): pl.pallas_call(attention_kernel, out_shape=(jax.ShapeDtypeStruct((length,...  32.9 us
    unnamed x9, local copies, waits for them, and re-layouts  7.4 us

profile of v5, /device:TPU:33, one launch (start us, length us, event | category | flops | bytes accessed | tf_op | source)
XLA Modules:
  0.0 163.6 jit_solution(3567681537968714837)
XLA Ops:
  0.6 51.3 %gather.1 = (f32[16,128,512]{2,1,0:T(8,128)}, bf16[16,128,1408]{2,1,0:T(8,128)(2,1)}, bf16[1408,1024]{1,0:T(8,128)(2,1)}, bf16[2048,256]{1,0:T(8,128)(2,1)}, s32[1,4]{1,0:T(1,128)}) custom-call(bf16[128,2688]{1,0:T(8,128)(2,1)} %tokens.1, bf16[336,256]{1,0:T(8,128)(2,1)} %wq.1, bf16[336,128]{1,0:T(8,128)(2,1)} %wk.1, bf16[336,128]{1,0:T(8,128)(2,1)} %wv.1, ...), custom_call_target="tpu_custom_call" | custom-call | tf_op jit(solution)/shard_map/gather/pallas_call | solution.py:492
  51.9 32.9 %attention.1 = (bf16[2048,256]{1,0:T(8,128)(2,1)}, bf16[2048,512]{1,0:T(8,128)(2,1)}) custom-call(s32[1,4]{1,0:T(1,128)} %docs_ref.1, s32[1,4]{1,0:T(1,128)} %get-tuple-element.12.docs2_ref, f32[2048,512]{1,0:T(8,128)} %bitcast.3, bf16[2048,256]{1,0:T(8,128)(2,1)} %cot_own.1, bf16[2048,256]{1,0:T(8,128)(2,1)} %get-tuple-element.14.cot_got, ...), custom_call_target="tpu_custom_call" | custom-call | tf_op jit(solution)/shard_map/attention/pallas_call | solution.py:223
  84.9 71.3 %scatter.1 = (bf16[128,4096]{1,0:T(8,128)(2,1)}, bf16[128,2688]{1,0:T(8,128)(2,1)}, f32[336,256]{1,0:T(8,128)}, f32[336,128]{1,0:T(8,128)}, f32[336,128]{1,0:T(8,128)}) custom-call(bf16[2048,256]{1,0:T(8,128)(2,1)} %get-tuple-element.15.attn, bf16[2048,512]{1,0:T(8,128)(2,1)} %get-tuple-element.16.dproj, bf16[16,128,1408]{2,1,0:T(8,128)(2,1)} %get-tuple-element.17.tok_in, ...), custom_call_target="tpu_custom_call" | custom-call | tf_op jit(solution)/shard_map/scatter/pallas_call | solution.py:695
  156.2 0.0 copy-start.1
  156.2 0.0 copy-start
  156.2 2.3 %copy.22 = bf16[128,4096]{1,0:T(8,128)(2,1)} copy(bf16[128,4096]{1,0:T(8,128)(2,1)} %get-tuple-element.24) | data formatting | bytes 2097152
  158.6 2.0 %copy.23 = bf16[128,2688]{1,0:T(8,128)(2,1)} copy(bf16[128,2688]{1,0:T(8,128)(2,1)} %get-tuple-element.25) | data formatting | bytes 1376256
  160.5 1.7 %copy.24 = f32[336,256]{1,0:T(8,128)} copy(f32[336,256]{1,0:T(8,128)} %get-tuple-element.26) | data formatting | bytes 688128
  162.3 0.0 copy-done.1
  162.3 0.7 copy.25
  162.9 0.0 copy-done
  163.0 0.7 copy.26
Async XLA Ops:
  156.2 6.1 %copy-start.1 = (f32[336,128]{1,0:T(8,128)S(1)}, f32[336,128]{1,0:T(8,128)}, u32[]{:S(2)}) copy-start(f32[336,128]{1,0:T(8,128)} %get-tuple-element.27) | copy-start | bytes 516100
  156.2 6.7 %copy-start = (f32[336,128]{1,0:T(8,128)S(1)}, f32[336,128]{1,0:T(8,128)}, u32[]{:S(2)}) copy-start(f32[336,128]{1,0:T(8,128)} %get-tuple-element.28) | copy-start | bytes 516100

commit v6 on v5

--- a/solution.py
+++ b/solution.py
@@ -531,7 +531,12 @@
     mine = pl.ds(pl.multiple_of(c * width, width), width)
     piece_rows = gq_out.shape[0]
 
-    pltpu.make_async_copy(w_in, w, local_s.at[4]).start()
+    for n, row in enumerate(order):
+        rows = pl.ds(pl.multiple_of(row * 512, 512), 512)
+        pltpu.make_async_copy(dproj.at[rows, :], dpj.at[rows, mine], local_s.at[n]).start()
+        if n == 0:
+            pltpu.make_async_copy(w_in, w, local_s.at[4]).start()
+    pltpu.make_async_copy(tok_in, tok, local_s.at[5]).start()
     meet(
         [me.sibling]
         + [
@@ -542,9 +547,7 @@
     )
     for n, row in enumerate(order):
         rows = pl.ds(pl.multiple_of(row * 512, 512), 512)
-        pltpu.make_async_copy(dproj.at[rows, :], dpj.at[rows, mine], local_s.at[n]).start()
         sends.send(dproj.at[rows, :], dpj.at[rows, mine], dp_s.at[n], me.sibling)
-    pltpu.make_async_copy(tok_in, tok, local_s.at[5]).start()
 
     def add(dst, *sources):
         total = dst[...].astype(jnp.float32)
@@ -652,16 +655,16 @@
             else:
                 sends.send(src, dst, attn_s.at[group], me.at(c=t, y=to_y, x=to_x))
 
-    for k in range(8):
-        arrive(rw.at[k], rw_s.at[k])
-    wsum[...] = summed(1 - t).astype(jnp.bfloat16)
-    sends.send(wsum, rwx, rwx_s.at[0], me.at(x=me.xp))
     for k, column in enumerate((x, me.xp)):
         arrive(rqx.at[3, k], qx_s.at[3, k])
         arrive(rq2.at[0, k], q2_s.at[0, k])
         arrive(rq2.at[1, k], q2_s.at[1, k])
         add(terms.at[own + column, q_rows, :], rqx.at[3, k], rq2.at[0, k], rq2.at[1, k])
     finish(1, q_rows)
+    for k in range(8):
+        arrive(rw.at[k], rw_s.at[k])
+    wsum[...] = summed(1 - t).astype(jnp.bfloat16)
+    sends.send(wsum, rwx, rwx_s.at[0], me.at(x=me.xp))
     for k, column in enumerate((x, me.xp)):
         arrive(rpx.at[k], px_s.at[k])
         add(terms.at[own + column, p_rows, :], rpx.at[k])
@@ -723,7 +726,7 @@
             dma((2,)), dma((2,)), dma((2, 2)), dma((8,)), dma((2, 2)), dma((1,)),
         ],
         compiler_params=pltpu.CompilerParams(
-            collective_id=1, has_side_effects=True, vmem_limit_bytes=60 * 1024 * 1024
+            collective_id=1, has_side_effects=True, vmem_limit_bytes=50 * 1024 * 1024
         ),
         name="scatter",
     )(attn, dproj, tok, w)

time: 165 us -> 165 us (level)
  local copies, waits for them, and re-layouts: 7.4 us -> 5.11 us
  Pallas kernels: 156 us -> 158 us
    unnamed x9 -> x7, local copies, waits for them, and re-layouts: 7.4 us -> 5.11 us
    pallas_call x1, Pallas kernels: 71.3 us -> 73.6 us  [scatter(): pl.pallas_call(scatter_kernel, out_shape=(jax.ShapeDtypeStruct((128, 32 *...]
where the time goes in v6:
time: 165 us; the launch traced here: 164 us
  Pallas kernels  158 us (96%)
  local copies, waits for them, and re-layouts  5.11 us (3%)
    pallas_call x1, Pallas kernels, scatter(): pl.pallas_call(scatter_kernel, out_shape=(jax.ShapeDtypeStruct((128, 32 *...  73.6 us
    pallas_call x1, Pallas kernels, gather(): pl.pallas_call(gather_kernel, out_shape=(jax.ShapeDtypeStruct((16, 128, 4...  51.3 us
    pallas_call x1, Pallas kernels, attention(): pl.pallas_call(attention_kernel, out_shape=(jax.ShapeDtypeStruct((length,...  32.9 us
    unnamed x7, local copies, waits for them, and re-layouts  5.11 us

profile of v6, /device:TPU:33, one launch (start us, length us, event | category | flops | bytes accessed | tf_op | source)
XLA Modules:
  0.0 163.6 jit_solution(16822634390982304284)
XLA Ops:
  0.6 51.3 %gather.1 = (f32[16,128,512]{2,1,0:T(8,128)}, bf16[16,128,1408]{2,1,0:T(8,128)(2,1)}, bf16[1408,1024]{1,0:T(8,128)(2,1)}, bf16[2048,256]{1,0:T(8,128)(2,1)}, s32[1,4]{1,0:T(1,128)}) custom-call(bf16[128,2688]{1,0:T(8,128)(2,1)} %tokens.1, bf16[336,256]{1,0:T(8,128)(2,1)} %wq.1, bf16[336,128]{1,0:T(8,128)(2,1)} %wk.1, bf16[336,128]{1,0:T(8,128)(2,1)} %wv.1, ...), custom_call_target="tpu_custom_call" | custom-call | tf_op jit(solution)/shard_map/gather/pallas_call | solution.py:492
  51.9 32.9 %attention.1 = (bf16[2048,256]{1,0:T(8,128)(2,1)}, bf16[2048,512]{1,0:T(8,128)(2,1)}) custom-call(s32[1,4]{1,0:T(1,128)} %docs_ref.1, s32[1,4]{1,0:T(1,128)} %get-tuple-element.12.docs2_ref, f32[2048,512]{1,0:T(8,128)} %bitcast.3, bf16[2048,256]{1,0:T(8,128)(2,1)} %cot_own.1, bf16[2048,256]{1,0:T(8,128)(2,1)} %get-tuple-element.14.cot_got, ...), custom_call_target="tpu_custom_call" | custom-call | tf_op jit(solution)/shard_map/attention/pallas_call | solution.py:223
  84.9 0.0 copy-start
  84.9 1.2 copy-done
  86.1 73.6 %scatter.1 = (bf16[128,4096]{1,0:T(8,128)(2,1)S(1)}, bf16[128,2688]{1,0:T(8,128)(2,1)S(1)}, f32[336,256]{1,0:T(8,128)S(1)}, f32[336,128]{1,0:T(8,128)S(1)}, f32[336,128]{1,0:T(8,128)S(1)}) custom-call(bf16[2048,256]{1,0:T(8,128)(2,1)S(1)} %copy-done, bf16[2048,512]{1,0:T(8,128)(2,1)} %get-tuple-element.16.dproj, ...), custom_call_target="tpu_custom_call" | custom-call | tf_op jit(solution)/shard_map/scatter/pallas_call | solution.py:698
  159.7 1.0 copy.22
  160.7 0.8 copy.23
  161.5 0.7 copy.24
  162.3 0.7 copy.25
  162.9 0.7 copy.26
Async XLA Ops:
  84.9 1.2 copy-start

commit v7 on v6

--- a/solution.py
+++ b/solution.py
@@ -56,7 +56,7 @@
 
 
 def attention_kernel(
-    docs_ref, docs2_ref, proj_hbm, cot_own, cot_got, cos_a, sin_a, cos_b, sin_b, gq_ref, gk_ref, out_hbm, dproj_hbm,
+    docs_ref, docs2_ref, proj_hbm, cot_own, cot_got, cos_a, sin_a, cos_b, sin_b, gq_ref, gk_ref, both_hbm,
     cot_ref, cot_sem, proj_ref, out_ref, dproj_ref, in_sem, out_sem, q_s, k_s, kt_s, v_s, vt_s, e_s, eb_s, dk_s, dv_s, acc_s, dot_s, row_s,
 ):
     length = proj_hbm.shape[0]
@@ -71,12 +71,12 @@
 
     def store(i, k):
         rows = block_rows(i)
-        src, dst, cols = (
-            (out_ref, out_hbm, pl.ds(0, 2 * HEAD)),
-            (dproj_ref, dproj_hbm, pl.ds(0, 2 * HEAD)),
-            (dproj_ref, dproj_hbm, pl.ds(2 * HEAD, 2 * HEAD)),
-        )[k]
-        return pltpu.make_async_copy(src.at[rows, cols], dst.at[rows, cols], out_sem.at[i, k])
+        src, low = ((out_ref, 0), (dproj_ref, 0), (dproj_ref, 2 * HEAD))[k]
+        return pltpu.make_async_copy(
+            src.at[rows, pl.ds(low, 2 * HEAD)],
+            both_hbm.at[rows, pl.ds(k * 2 * HEAD, 2 * HEAD)],
+            out_sem.at[i, k],
+        )
 
     for i in range(blocks):
         load(i).start()
@@ -222,14 +222,11 @@
     bf, f32 = jnp.bfloat16, jnp.float32
     return pl.pallas_call(
         attention_kernel,
-        out_shape=(
-            jax.ShapeDtypeStruct((length, 2 * HEAD), bf),
-            jax.ShapeDtypeStruct((length, 4 * HEAD), bf),
-        ),
+        out_shape=jax.ShapeDtypeStruct((length, 6 * HEAD), bf),
         in_specs=[pl.BlockSpec(memory_space=pltpu.SMEM)] * 2
         + [pl.BlockSpec(memory_space=pl.ANY)] * 3
         + [vmem] * 6,
-        out_specs=(pl.BlockSpec(memory_space=pl.ANY), pl.BlockSpec(memory_space=pl.ANY)),
+        out_specs=pl.BlockSpec(memory_space=pl.ANY),
         scratch_shapes=[
             pltpu.VMEM((length, 2 * HEAD), bf),
             pltpu.SemaphoreType.DMA(()),
@@ -518,7 +515,7 @@
 
 
 def scatter_kernel(
-    attn, dproj, tok_in, w_in, attn_out, token_out, gq_out, gk_out, gv_out,
+    both, tok_in, w_in, attn_out, token_out, gq_out, gk_out, gv_out,
     tok, w, dpj, terms, dw, rqx, rp1, rp2, rpx, rq1, rq2, rw, rwx, wsum, grad_out,
     send_s, attn_s, dp_s, local_s, qx_s, p1_s, p2_s, px_s, q1_s, q2_s, rw_s, g_s, rwx_s,
 ):
@@ -531,6 +528,7 @@
     mine = pl.ds(pl.multiple_of(c * width, width), width)
     piece_rows = gq_out.shape[0]
 
+    attn, dproj = both.at[:, pl.ds(0, 2 * HEAD)], both.at[:, pl.ds(2 * HEAD, width)]
     for n, row in enumerate(order):
         rows = pl.ds(pl.multiple_of(row * 512, 512), 512)
         pltpu.make_async_copy(dproj.at[rows, :], dpj.at[rows, mine], local_s.at[n]).start()
@@ -688,12 +686,12 @@
     sends.finish()
 
 
-def scatter(attn, dproj, tok, w, piece_rows):
+def scatter(both, tok, w, piece_rows):
     f32, bf = jnp.float32, jnp.bfloat16
     anywhere = pl.BlockSpec(memory_space=pl.ANY)
     vmem = pl.BlockSpec(memory_space=pltpu.VMEM)
     dma = pltpu.SemaphoreType.DMA
-    length = attn.shape[0]
+    length = both.shape[0]
     half = (HALF_ROWS, KH)
     return pl.pallas_call(
         scatter_kernel,
@@ -704,7 +702,7 @@
             jax.ShapeDtypeStruct((piece_rows, HEAD), f32),
             jax.ShapeDtypeStruct((piece_rows, HEAD), f32),
         ),
-        in_specs=[anywhere] * 4,
+        in_specs=[anywhere] * 3,
         out_specs=(anywhere, vmem, vmem, vmem, vmem),
         scratch_shapes=[
             pltpu.VMEM((16, 128, KH), bf),
@@ -729,7 +727,7 @@
             collective_id=1, has_side_effects=True, vmem_limit_bytes=50 * 1024 * 1024
         ),
         name="scatter",
-    )(attn, dproj, tok, w)
+    )(both, tok, w)
 
 
 def local(
@@ -739,10 +737,10 @@
         tokens, q_weight, key_projection, value_projection, out_cot, doc_lengths
     )
     proj = proj.reshape(out_cot.shape[0], 4 * HEAD)
-    attn, dproj = attention(
+    both = attention(
         doc_lengths, docs2, proj, out_cot, cot2, query_norm_gain, key_norm_gain
     )
-    attn_out, token_grad, gq, gk, gv = scatter(attn, dproj, tok, w, q_weight.shape[0])
+    attn_out, token_grad, gq, gk, gv = scatter(both, tok, w, q_weight.shape[0])
     return (attn_out, token_grad, gq, gk, gv)
 
 

time: 165 us -> 165 us (level); the launches traced: 164 us -> 162 us
    unnamed x7 -> x5, local copies, waits for them, and re-layouts: 5.11 us -> 3.89 us
where the time goes in v7:
time: 165 us; the launch traced here: 162 us
  Pallas kernels  157 us (95%)
  local copies, waits for them, and re-layouts  3.89 us (2%)
    pallas_call x1, Pallas kernels, scatter(): pl.pallas_call(scatter_kernel, out_shape=(jax.ShapeDtypeStruct((128, 32 *...  73 us
    pallas_call x1, Pallas kernels, gather(): pl.pallas_call(gather_kernel, out_shape=(jax.ShapeDtypeStruct((16, 128, 4...  51.3 us
    pallas_call x1, Pallas kernels, attention(): pl.pallas_call(attention_kernel, out_shape=jax.ShapeDtypeStruct((length,...  32.9 us
    unnamed x5, local copies, waits for them, and re-layouts  3.89 us

profile of v7, /device:TPU:33, one launch (start us, length us, event | category | flops | bytes accessed | tf_op | source)
XLA Modules:
  0.0 161.8 jit_solution(7497029995876753095)
XLA Ops:
  0.6 51.3 %gather.1 = (f32[16,128,512]{2,1,0:T(8,128)}, bf16[16,128,1408]{2,1,0:T(8,128)(2,1)}, bf16[1408,1024]{1,0:T(8,128)(2,1)}, bf16[2048,256]{1,0:T(8,128)(2,1)}, s32[1,4]{1,0:T(1,128)}) custom-call(bf16[128,2688]{1,0:T(8,128)(2,1)} %tokens.1, bf16[336,256]{1,0:T(8,128)(2,1)} %wq.1, bf16[336,128]{1,0:T(8,128)(2,1)} %wk.1, bf16[336,128]{1,0:T(8,128)(2,1)} %wv.1, ...), custom_call_target="tpu_custom_call" | custom-call | tf_op jit(solution)/shard_map/gather/pallas_call | solution.py:489
  51.9 32.9 %attention.1.both = bf16[2048,768]{1,0:T(8,128)(2,1)} custom-call(s32[1,4]{1,0:T(1,128)} %docs_ref.1, s32[1,4]{1,0:T(1,128)} %get-tuple-element.10.docs2_ref, f32[2048,512]{1,0:T(8,128)} %bitcast.3, bf16[2048,256]{1,0:T(8,128)(2,1)} %cot_own.1, bf16[2048,256]{1,0:T(8,128)(2,1)} %get-tuple-element.12.cot_got, f32[8,128]{1,0:T(8,128)} %constant.8.clone.cos_a, ...), custom_call_target="tpu_custom_call" | custom-call | tf_op jit(solution)/shard_map/attention/pallas_call | solution.py:223
  84.9 73.0 %scatter.1 = (bf16[128,4096]{1,0:T(8,128)(2,1)S(1)}, bf16[128,2688]{1,0:T(8,128)(2,1)S(1)}, f32[336,256]{1,0:T(8,128)S(1)}, f32[336,128]{1,0:T(8,128)S(1)}, f32[336,128]{1,0:T(8,128)S(1)}) custom-call(bf16[2048,768]{1,0:T(8,128)(2,1)} %attention.1.both, bf16[16,128,1408]{2,1,0:T(8,128)(2,1)} %get-tuple-element.13.tok_in, ...), custom_call_target="tpu_custom_call" | custom-call | tf_op jit(solution)/shard_map/scatter/pallas_call | solution.py:696
  157.9 1.0 copy.22
  158.8 0.8 copy.23
  159.7 0.7 copy.24
  160.4 0.7 copy.25
  161.1 0.7 copy.26

commit v8 on v7

--- a/solution.py
+++ b/solution.py
@@ -602,6 +602,20 @@
     far, up, down, own = me.far_y * 4, me.up_y * 4, me.down_y * 4, y * 4
     group = y * 4 + jnp.where(same, x, me.xp)
     columns = pl.ds(pl.multiple_of(group * 2 * HEAD, 2 * HEAD), 2 * HEAD)
+    for dy in range(4):
+        for dx in range(4):
+            to_y, to_x = (y + dy) % 4, (x + dx) % 4
+            rows = pl.ds(pl.multiple_of((to_y * 4 + to_x) * 128, 128), 128)
+            src, dst = attn.at[rows, :], attn_out.at[:, columns]
+            if dy == 0 and dx == 0:
+                sends.send(src, dst, attn_s.at[group], me.sibling, when=jnp.logical_not(same))
+
+                @pl.when(same)
+                def _():
+                    pltpu.make_async_copy(src, dst, attn_s.at[group]).start()
+            else:
+                sends.send(src, dst, attn_s.at[group], me.at(c=t, y=to_y, x=to_x))
+
     compute(0)
     sends.send(terms.at[pl.ds(far, 2), p_rows, :], rp1.at[0], p1_s.at[0], me.up)
     sends.send(terms.at[pl.ds(far + 2, 2), p_rows, :], rp1.at[1], p1_s.at[1], me.down)
@@ -638,20 +652,6 @@
         for k in range(1, 4):
             total = total + rw[2 * k + g].astype(jnp.float32)
         return total
-
-    for dy in range(4):
-        for dx in range(4):
-            to_y, to_x = (y + dy) % 4, (x + dx) % 4
-            rows = pl.ds(pl.multiple_of((to_y * 4 + to_x) * 128, 128), 128)
-            src, dst = attn.at[rows, :], attn_out.at[:, columns]
-            if dy == 0 and dx == 0:
-                sends.send(src, dst, attn_s.at[group], me.sibling, when=jnp.logical_not(same))
-
-                @pl.when(same)
-                def _():
-                    pltpu.make_async_copy(src, dst, attn_s.at[group]).start()
-            else:
-                sends.send(src, dst, attn_s.at[group], me.at(c=t, y=to_y, x=to_x))
 
     for k, column in enumerate((x, me.xp)):
         arrive(rqx.at[3, k], qx_s.at[3, k])

time: 165 us -> 165 us (level)
  Pallas kernels: 157 us -> 159 us
where the time goes in v8:
time: 165 us; the launch traced here: 163 us
  Pallas kernels  159 us (96%)
  local copies, waits for them, and re-layouts  3.89 us (2%)
    pallas_call x1, Pallas kernels, scatter(): pl.pallas_call(scatter_kernel, out_shape=(jax.ShapeDtypeStruct((128, 32 *...  74.5 us
    pallas_call x1, Pallas kernels, gather(): pl.pallas_call(gather_kernel, out_shape=(jax.ShapeDtypeStruct((16, 128, 4...  51.3 us
    pallas_call x1, Pallas kernels, attention(): pl.pallas_call(attention_kernel, out_shape=jax.ShapeDtypeStruct((length,...  32.9 us
    unnamed x5, local copies, waits for them, and re-layouts  3.89 us

profile of v8, /device:TPU:33, one launch (start us, length us, event | category | flops | bytes accessed | tf_op | source)
XLA Modules:
  0.0 163.3 jit_solution(6635718038143940767)
XLA Ops:
  0.6 51.3 %gather.1 = (f32[16,128,512]{2,1,0:T(8,128)}, bf16[16,128,1408]{2,1,0:T(8,128)(2,1)}, bf16[1408,1024]{1,0:T(8,128)(2,1)}, bf16[2048,256]{1,0:T(8,128)(2,1)}, s32[1,4]{1,0:T(1,128)}) custom-call(bf16[128,2688]{1,0:T(8,128)(2,1)} %tokens.1, bf16[336,256]{1,0:T(8,128)(2,1)} %wq.1, bf16[336,128]{1,0:T(8,128)(2,1)} %wk.1, bf16[336,128]{1,0:T(8,128)(2,1)} %wv.1, ...), custom_call_target="tpu_custom_call" | custom-call | tf_op jit(solution)/shard_map/gather/pallas_call | solution.py:489
  51.9 32.9 %attention.1.both = bf16[2048,768]{1,0:T(8,128)(2,1)} custom-call(s32[1,4]{1,0:T(1,128)} %docs_ref.1, s32[1,4]{1,0:T(1,128)} %get-tuple-element.10.docs2_ref, f32[2048,512]{1,0:T(8,128)} %bitcast.3, bf16[2048,256]{1,0:T(8,128)(2,1)} %cot_own.1, bf16[2048,256]{1,0:T(8,128)(2,1)} %get-tuple-element.12.cot_got, f32[8,128]{1,0:T(8,128)} %constant.8.clone.cos_a, ...), custom_call_target="tpu_custom_call" | custom-call | tf_op jit(solution)/shard_map/attention/pallas_call | solution.py:223
  84.9 74.5 %scatter.1 = (bf16[128,4096]{1,0:T(8,128)(2,1)S(1)}, bf16[128,2688]{1,0:T(8,128)(2,1)S(1)}, f32[336,256]{1,0:T(8,128)S(1)}, f32[336,128]{1,0:T(8,128)S(1)}, f32[336,128]{1,0:T(8,128)S(1)}) custom-call(bf16[2048,768]{1,0:T(8,128)(2,1)} %attention.1.both, bf16[16,128,1408]{2,1,0:T(8,128)(2,1)} %get-tuple-element.13.tok_in, ...), custom_call_target="tpu_custom_call" | custom-call | tf_op jit(solution)/shard_map/scatter/pallas_call | solution.py:696
  159.4 1.0 copy.22
  160.3 0.8 copy.23
  161.2 0.7 copy.24
  161.9 0.7 copy.25
  162.6 0.7 copy.26
